TPU v7x, 512 devices: a whole 4x8x8 slice. The times are simulated.
512 devices in a mesh: seq: 64 (over y, x, core), ch: 8 (over z).
Axes of the slice: x: 4, y: 8, z: 8, core: 2. Of those that a mesh axis runs over, the one named last changes fastest.
Arguments:
- inputs: bfloat16 [256, 32768], P('ch', 'seq'), may hold values from -6 to 6
- proj_weight: bfloat16 [3, 256, 256], P(None, 'ch'), may hold values from -0.5 to 0.5
- short_taps: float32 [256, 3, 3], P('ch'), may hold values from -3 to 3
- skip_gain: float32 [256, 2], P('ch'), may hold values from -1 to 1
- filters: float32 [2, 256, 32768], P(None, 'ch', 'seq'), may hold values from -1 to 1
- out_weight: bfloat16 [256, 256], P('ch'), may hold values from -0.5 to 0.5
Outputs:
- outputs: bfloat16 [256, 32768], P('ch', 'seq')
All inputs are finite; a program needn't handle non-finite values.
Results may differ from a plain program's by a relative error of at most 0.007.
Values may be sent and summed in bfloat16 or wider, within the bound.
No kernel may reach another device: no remote copies, remote signals or barrier semaphores. Data moves between devices by JAX's collectives and lax.ppermute only.
A program may use at most 64 MiB of HBM per device.

v0:
```python
import math

import jax
import jax.numpy as jnp
from jax import lax
from jax.sharding import PartitionSpec as P

highest = lax.Precision.HIGHEST


def swapped(block, axis, stride):
    count = lax.axis_size(axis)
    route = []
    for low in range(count):
        high = low | 1 << stride
        if high != low and high < count:
            route += [(low, high), (high, low)]
    return lax.ppermute(block, axis, route)


def passed_along(shard, axis, by):
    size = lax.axis_size(axis)
    pairs = [(i, i + by) for i in range(size) if 0 <= i + by < size]
    return lax.ppermute(shard, axis, pairs)


def reversed_bits(device, levels):
    result = jnp.zeros((), jnp.int32)
    for level in range(levels):
        result = result | (device >> level & 1) << levels - 1 - level
    return result


def complex_product(left, right):
    return jnp.stack(
        [left[0] * right[0] - left[1] * right[1], left[0] * right[1] + left[1] * right[0]]
    )


def twiddle(spectrum, first_row, total, undo):
    length = spectrum.shape[-1]
    column = jnp.arange(length, dtype=jnp.int32)
    row_index = first_row + jnp.arange(2, dtype=jnp.int32)
    angle = (
        2.0 * math.pi / total * (row_index[:, None] * column[None, :] % total).astype(jnp.float32)
    )
    cosine = jnp.cos(angle)
    sine = jnp.sin(angle)
    real_part = spectrum[0]
    imag_part = spectrum[1]
    if undo:
        return jnp.stack(
            [real_part * cosine - imag_part * sine, real_part * sine + imag_part * cosine]
        )
    return jnp.stack([real_part * cosine + imag_part * sine, imag_part * cosine - real_part * sine])


def local_dft(spectrum, undo):
    length = spectrum.shape[-1]
    width = min(128, length)
    column = jnp.arange(length, dtype=jnp.int32)
    blocks = []
    for block in range(length // width):
        target = block * width + jnp.arange(width, dtype=jnp.int32)
        angle = (
            2.0
            * math.pi
            / length
            * (column[:, None] * target[None, :] % length).astype(jnp.float32)
        )
        table = jnp.stack([jnp.cos(angle), jnp.sin(angle)])
        products = jnp.einsum("xrem,ymd->xyred", spectrum, table, precision=highest)
        if undo:
            blocks.append(
                jnp.stack([products[0, 0] - products[1, 1], products[0, 1] + products[1, 0]])
            )
        else:
            blocks.append(
                jnp.stack([products[0, 0] + products[1, 1], products[1, 0] - products[0, 1]])
            )
    return jnp.concatenate(blocks, axis=-1)


def forward(signal):
    count = lax.axis_size("seq")
    device = lax.axis_index("seq")
    length = signal.shape[-1]
    total = 2 * count * length
    levels = count.bit_length() - 1
    phase = math.pi / count * device.astype(jnp.float32)
    real_rows = jnp.stack([signal, signal * jnp.cos(phase)], axis=1)
    imag_rows = jnp.stack([jnp.zeros_like(signal), -signal * jnp.sin(phase)], axis=1)
    state = jnp.stack([real_rows, imag_rows])
    for level in reversed(range(levels)):
        half = 1 << level
        partner = swapped(state, "seq", level)
        upper = device >> level & 1 == 1
        angle = math.pi / half * (device & half - 1).astype(jnp.float32)
        cosine = jnp.cos(angle)
        sine = jnp.sin(angle)
        diff_real = partner[0] - state[0]
        diff_imag = partner[1] - state[1]
        turned = jnp.stack(
            [diff_real * cosine + diff_imag * sine, diff_imag * cosine - diff_real * sine]
        )
        state = jnp.where(upper, turned, state + partner)
    first_row = 2 * reversed_bits(device, levels)
    return local_dft(twiddle(state, first_row, total, False), False)


def inverse(spectrum):
    count = lax.axis_size("seq")
    device = lax.axis_index("seq")
    length = spectrum.shape[-1]
    total = 2 * count * length
    levels = count.bit_length() - 1
    first_row = 2 * reversed_bits(device, levels)
    state = twiddle(local_dft(spectrum, True), first_row, total, True)
    for level in range(levels):
        half = 1 << level
        partner = swapped(state, "seq", level)
        upper = device >> level & 1 == 1
        angle = math.pi / half * (device & half - 1).astype(jnp.float32)
        cosine = jnp.cos(angle)
        sine = jnp.sin(angle)
        own_turned = jnp.stack(
            [state[0] * cosine - state[1] * sine, state[0] * sine + state[1] * cosine]
        )
        partner_turned = jnp.stack(
            [partner[0] * cosine - partner[1] * sine, partner[0] * sine + partner[1] * cosine]
        )
        state = jnp.where(upper, partner - own_turned, state + partner_turned)
    phase = math.pi / count * device.astype(jnp.float32)
    result = state[0][:, 0] + jnp.cos(phase) * state[0][:, 1] - jnp.sin(phase) * state[1][:, 1]
    return result * (1.0 / total)


def local(inputs, proj_weight, short_taps, skip_gain, filters, out_weight):
    channels = inputs.shape[0]
    length = inputs.shape[1]
    columns = proj_weight
    summed = lax.psum_scatter(
        jnp.einsum("sio,it->ost", columns, inputs, preferred_element_type=jnp.float32),
        "ch",
        scatter_dimension=0,
        tiled=True,
    )
    projected = summed.astype(jnp.bfloat16)
    before = passed_along(projected[:, :, length - 2 :], "seq", 1)
    padded = jnp.concatenate([before, projected], axis=2).astype(jnp.float32)
    conv_in = (
        short_taps[:, :, 0:1] * padded[:, :, 2:]
        + short_taps[:, :, 1:2] * padded[:, :, 1:-1]
        + short_taps[:, :, 2:3] * padded[:, :, :-2]
    )
    values = conv_in[:, 0, :]
    first_gate = conv_in[:, 1, :]
    second_gate = conv_in[:, 2, :]
    spectra = forward(jnp.concatenate([values, filters[0], filters[1]], axis=0))
    value_spectrum = spectra[:, :channels]
    first_filter = spectra[:, channels : 2 * channels]
    second_filter = spectra[:, 2 * channels :]
    first = inverse(complex_product(value_spectrum, first_filter)) + skip_gain[:, 0:1] * values
    gated = first_gate * first
    second = inverse(complex_product(forward(gated), second_filter)) + skip_gain[:, 1:2] * gated
    mixed = (second_gate * second).astype(jnp.bfloat16)
    columns = out_weight
    result = lax.psum_scatter(
        jnp.einsum("io,it->ot", columns, mixed, preferred_element_type=jnp.float32),
        "ch",
        scatter_dimension=0,
        tiled=True,
    )
    return result.astype(jnp.bfloat16)


def solution(mesh):
    in_specs = (
        P("ch", "seq"),
        P(None, "ch", None),
        P("ch", None, None),
        P("ch", None),
        P(None, "ch", "seq"),
        P("ch", None),
    )
    out_specs = P("ch", "seq")
    return jax.shard_map(local, mesh=mesh, in_specs=in_specs, out_specs=out_specs, check_vma=False)
```

profile of v0, /device:TPU:1, one launch (start us, length us, event | category | flops | bytes accessed | tf_op | source)
XLA Modules:
  0.0 494.5 jit_solution(9529714887624001466)
XLA Ops:
  11.8 62.7 %all-reduce.4 = bf16[256,3,512]{2,1,0:T(4,128)(2,1)S(1)} all-reduce(f32[256,3,512]{2,1,0:T(4,128)S(1)} %copy.76), channel_id=2, replica_groups=mesh['seq'=64,'ch'=8] {'ch'}, use_global_device_ids=true, to_apply=%region_0.0.clone | all-reduce | flops 393216 | bytes 2359296
  76.6 14.3 %collective-permute-start = (bf16[32,3,2]{2,1,0:T(4,128)(2,1)S(1)}, bf16[32,3,2]{2,1,0:T(4,128)(2,1)S(1)}, u32[]{:S(2)}, u32[]{:S(2)}) collective-permute-start(bf16[32,3,2]{2,1,0:T(4,128)(2,1)S(1)} %slice.834), channel_id=1, source_target_pairs={{0,8},{8,16},{16,24},{24,32},{32,40},{40,48},{48,56},{56,64},{64,7... | collective-permute-start | bytes 1160 | tf_op jit(solution)/shard_map/ppermute | solution.py:24
  92.5 7.4 %collective-permute-start.1 = (f32[2,96,2,512]{3,1,2,0:T(8,128)S(1)}, f32[2,96,2,512]{3,1,2,0:T(8,128)S(1)}, u32[]{:S(2)}, u32[]{:S(2)}) collective-permute-start(f32[2,96,2,512]{3,1,2,0:T(8,128)S(1)} %pad_maximum_fusion), channel_id=1, source_target_pairs={{0,256},{256,0},{8,264},{264,8},{16,272},{272,16},{24,280},{280,24... | collective-permute-start | bytes 2359304 | tf_op jit(solution)/shard_map/ppermute | solution.py:18
  100.1 18.1 %collective-permute-done.1 = f32[2,96,2,512]{3,1,2,0:T(8,128)S(1)} collective-permute-done((f32[2,96,2,512]{3,1,2,0:T(8,128)S(1)}, f32[2,96,2,512]{3,1,2,0:T(8,128)S(1)}, u32[]{:S(2)}, u32[]{:S(2)}) %collective-permute-start.1) | collective-permute-done | bytes 786464 | tf_op jit(solution)/shard_map/ppermute | solution.py:18
  119.5 20.6 %collective-permute-start.2 = (f32[2,96,2,512]{3,1,2,0:T(8,128)}, f32[2,96,2,512]{3,1,2,0:T(8,128)S(1)}, u32[]{:S(2)}, u32[]{:S(2)}) collective-permute-start(f32[2,96,2,512]{3,1,2,0:T(8,128)} %maximum_select_fusion), channel_id=1, source_target_pairs={{0,128},{128,0},{8,136},{136,8},{16,144},{144,16},{24,152},{152,24... | collective-permute-start | bytes 2359304 | tf_op jit(solution)/shard_map/ppermute | solution.py:18
  140.3 34.5 %collective-permute-done.2 = f32[2,96,2,512]{3,1,2,0:T(8,128)S(1)} collective-permute-done((f32[2,96,2,512]{3,1,2,0:T(8,128)}, f32[2,96,2,512]{3,1,2,0:T(8,128)S(1)}, u32[]{:S(2)}, u32[]{:S(2)}) %collective-permute-start.2) | collective-permute-done | bytes 786464 | tf_op jit(solution)/shard_map/ppermute | solution.py:18
  180.1 18.4 %collective-permute-done.3 = f32[2,96,2,512]{3,1,2,0:T(8,128)S(1)} collective-permute-done((f32[2,96,2,512]{3,1,2,0:T(8,128)S(1)}, f32[2,96,2,512]{3,1,2,0:T(8,128)S(1)}, u32[]{:S(2)}, u32[]{:S(2)}) %collective-permute-start.3) | collective-permute-done | bytes 786464 | tf_op jit(solution)/shard_map/ppermute | solution.py:18
  201.7 18.4 %collective-permute-done.4 = f32[2,96,2,512]{3,1,2,0:T(8,128)S(1)} collective-permute-done((f32[2,96,2,512]{3,1,2,0:T(8,128)S(1)}, f32[2,96,2,512]{3,1,2,0:T(8,128)S(1)}, u32[]{:S(2)}, u32[]{:S(2)}) %collective-permute-start.4) | collective-permute-done | bytes 786464 | tf_op jit(solution)/shard_map/ppermute | solution.py:18
  223.9 15.5 %collective-permute-done.5 = f32[2,96,2,512]{3,1,2,0:T(8,128)S(1)} collective-permute-done((f32[2,96,2,512]{3,1,2,0:T(8,128)S(1)}, f32[2,96,2,512]{3,1,2,0:T(8,128)S(1)}, u32[]{:S(2)}, u32[]{:S(2)}) %collective-permute-start.5) | collective-permute-done | bytes 786464 | tf_op jit(solution)/shard_map/ppermute | solution.py:18
  259.7 7.7 %collective-permute-done.8 = f32[2,32,2,512]{3,1,2,0:T(8,128)S(1)} collective-permute-done((f32[2,32,2,512]{3,1,2,0:T(8,128)S(1)}, f32[2,32,2,512]{3,1,2,0:T(8,128)S(1)}, u32[]{:S(2)}, u32[]{:S(2)}) %collective-permute-start.8) | collective-permute-done | bytes 262176 | tf_op jit(solution)/shard_map/ppermute | solution.py:18
  270.2 7.6 %collective-permute-done.9 = f32[2,32,2,512]{3,1,2,0:T(8,128)S(1)} collective-permute-done((f32[2,32,2,512]{3,1,2,0:T(8,128)S(1)}, f32[2,32,2,512]{3,1,2,0:T(8,128)S(1)}, u32[]{:S(2)}, u32[]{:S(2)}) %collective-permute-start.9) | collective-permute-done | bytes 262176 | tf_op jit(solution)/shard_map/ppermute | solution.py:18
  290.7 11.7 %collective-permute-done.11 = f32[2,32,2,512]{3,1,2,0:T(8,128)S(1)} collective-permute-done((f32[2,32,2,512]{3,1,2,0:T(8,128)S(1)}, f32[2,32,2,512]{3,1,2,0:T(8,128)S(1)}, u32[]{:S(2)}, u32[]{:S(2)}) %collective-permute-start.11) | collective-permute-done | bytes 262176 | tf_op jit(solution)/shard_map/ppermute | solution.py:18
  307.4 14.6 %collective-permute-done.12 = f32[2,32,2,512]{3,1,2,0:T(8,128)S(1)} collective-permute-done((f32[2,32,2,512]{3,1,2,0:T(8,128)S(1)}, f32[2,32,2,512]{3,1,2,0:T(8,128)S(1)}, u32[]{:S(2)}, u32[]{:S(2)}) %collective-permute-start.12) | collective-permute-done | bytes 262176 | tf_op jit(solution)/shard_map/ppermute | solution.py:18
  326.7 8.7 %collective-permute-done.13 = f32[2,32,2,512]{3,1,2,0:T(8,128)S(1)} collective-permute-done((f32[2,32,2,512]{3,1,2,0:T(8,128)S(1)}, f32[2,32,2,512]{3,1,2,0:T(8,128)S(1)}, u32[]{:S(2)}, u32[]{:S(2)}) %collective-permute-start.13) | collective-permute-done | bytes 262176 | tf_op jit(solution)/shard_map/ppermute | solution.py:18
  337.5 13.7 %collective-permute-done.14 = f32[2,32,2,512]{3,1,2,0:T(8,128)S(1)} collective-permute-done((f32[2,32,2,512]{3,1,2,0:T(8,128)S(1)}, f32[2,32,2,512]{3,1,2,0:T(8,128)S(1)}, u32[]{:S(2)}, u32[]{:S(2)}) %collective-permute-start.14) | collective-permute-done | bytes 262176 | tf_op jit(solution)/shard_map/ppermute | solution.py:18
  353.3 6.4 %collective-permute-done.15 = f32[2,32,2,512]{3,1,2,0:T(8,128)S(1)} collective-permute-done((f32[2,32,2,512]{3,1,2,0:T(8,128)S(1)}, f32[2,32,2,512]{3,1,2,0:T(8,128)S(1)}, u32[]{:S(2)}, u32[]{:S(2)}) %collective-permute-start.15) | collective-permute-done | bytes 262176 | tf_op jit(solution)/shard_map/ppermute | solution.py:18
  376.1 6.2 %collective-permute-start.18 = (f32[2,32,2,512]{3,1,2,0:T(8,128)S(1)}, f32[2,32,2,512]{3,1,2,0:T(8,128)S(1)}, u32[]{:S(2)}, u32[]{:S(2)}) collective-permute-start(f32[2,32,2,512]{3,1,2,0:T(8,128)S(1)} %maximum_select_fusion.10), channel_id=1, source_target_pairs={{0,8},{8,0},{16,24},{24,16},{32,40},{40,32},{48,56},{56,48},{64,72... | collective-permute-start | bytes 786440 | tf_op jit(solution)/shard_map/ppermute | solution.py:18
  393.6 6.9 %collective-permute-done.20 = f32[2,32,2,512]{3,1,2,0:T(8,128)S(1)} collective-permute-done((f32[2,32,2,512]{3,1,2,0:T(8,128)S(1)}, f32[2,32,2,512]{3,1,2,0:T(8,128)S(1)}, u32[]{:S(2)}, u32[]{:S(2)}) %collective-permute-start.20) | collective-permute-done | bytes 262176 | tf_op jit(solution)/shard_map/ppermute | solution.py:18
  404.5 6.2 %collective-permute-done.21 = f32[2,32,2,512]{3,1,2,0:T(8,128)S(1)} collective-permute-done((f32[2,32,2,512]{3,1,2,0:T(8,128)S(1)}, f32[2,32,2,512]{3,1,2,0:T(8,128)S(1)}, u32[]{:S(2)}, u32[]{:S(2)}) %collective-permute-start.21) | collective-permute-done | bytes 262176 | tf_op jit(solution)/shard_map/ppermute | solution.py:18
  413.1 5.4 %collective-permute-done.22 = f32[2,32,2,512]{3,1,2,0:T(8,128)S(1)} collective-permute-done((f32[2,32,2,512]{3,1,2,0:T(8,128)S(1)}, f32[2,32,2,512]{3,1,2,0:T(8,128)S(1)}, u32[]{:S(2)}, u32[]{:S(2)}) %collective-permute-start.22) | collective-permute-done | bytes 262176 | tf_op jit(solution)/shard_map/ppermute | solution.py:18
  423.0 11.7 %collective-permute-done.23 = f32[2,32,2,512]{3,1,2,0:T(8,128)S(1)} collective-permute-done((f32[2,32,2,512]{3,1,2,0:T(8,128)S(1)}, f32[2,32,2,512]{3,1,2,0:T(8,128)S(1)}, u32[]{:S(2)}, u32[]{:S(2)}) %collective-permute-start.23) | collective-permute-done | bytes 262176 | tf_op jit(solution)/shard_map/ppermute | solution.py:18
  434.9 7.0 %collective-permute-start.24 = (f32[2,32,2,512]{3,1,2,0:T(8,128)S(1)}, f32[2,32,2,512]{3,1,2,0:T(8,128)S(1)}, u32[]{:S(2)}, u32[]{:S(2)}) collective-permute-start(f32[2,32,2,512]{3,1,2,0:T(8,128)S(1)} %fusion.44), channel_id=1, source_target_pairs={{0,256},{256,0},{8,264},{264,8},{16,272},{272,16},{24,280},{280,24... | collective-permute-start | bytes 786440 | tf_op jit(solution)/shard_map/ppermute | solution.py:18
  442.0 8.5 %collective-permute-done.24 = f32[2,32,2,512]{3,1,2,0:T(8,128)S(1)} collective-permute-done((f32[2,32,2,512]{3,1,2,0:T(8,128)S(1)}, f32[2,32,2,512]{3,1,2,0:T(8,128)S(1)}, u32[]{:S(2)}, u32[]{:S(2)}) %collective-permute-start.24) | collective-permute-done | bytes 262176 | tf_op jit(solution)/shard_map/ppermute | solution.py:18
  452.0 34.2 %reduce-scatter.4.cloned.1.call-done = f32[32,512]{1,0:T(8,128)} async-done(((f32[256,512]{1,0:T(8,128)}), f32[32,512]{1,0:T(8,128)}) %reduce-scatter.4.cloned.1.call-update) | async-done | bytes 65552 | tf_op jit(solution)/shard_map/reduce_scatter | solution.py:168
  (186 shorter events, 111.7 us)
Async XLA Ops:
  6.5 479.6 %reduce-scatter.4.cloned.1.call-start = ((), (), s32[]{:S(2)}) async-start(), calls=%async_computation.1 | async-start | bytes 589824 | tf_op jit(solution)/shard_map/reduce_scatter | solution.py:168
  76.6 15.3 %collective-permute-start = (bf16[32,3,2]{2,1,0:T(4,128)(2,1)S(1)}, bf16[32,3,2]{2,1,0:T(4,128)(2,1)S(1)}, u32[]{:S(2)}, u32[]{:S(2)}) collective-permute-start(bf16[32,3,2]{2,1,0:T(4,128)(2,1)S(1)} %slice.834), channel_id=1, source_target_pairs={{0,8},{8,16},{16,24},{24,32},{32,40},{40,48},{48,56},{56,64},{64,7... | collective-permute-start | bytes 1160 | tf_op jit(solution)/shard_map/ppermute | solution.py:24
  92.5 25.7 %collective-permute-start.1 = (f32[2,96,2,512]{3,1,2,0:T(8,128)S(1)}, f32[2,96,2,512]{3,1,2,0:T(8,128)S(1)}, u32[]{:S(2)}, u32[]{:S(2)}) collective-permute-start(f32[2,96,2,512]{3,1,2,0:T(8,128)S(1)} %pad_maximum_fusion), channel_id=1, source_target_pairs={{0,256},{256,0},{8,264},{264,8},{16,272},{272,16},{24,280},{280,24... | collective-permute-start | bytes 2359304 | tf_op jit(solution)/shard_map/ppermute | solution.py:18
  119.5 55.3 %collective-permute-start.2 = (f32[2,96,2,512]{3,1,2,0:T(8,128)}, f32[2,96,2,512]{3,1,2,0:T(8,128)S(1)}, u32[]{:S(2)}, u32[]{:S(2)}) collective-permute-start(f32[2,96,2,512]{3,1,2,0:T(8,128)} %maximum_select_fusion), channel_id=1, source_target_pairs={{0,128},{128,0},{8,136},{136,8},{16,144},{144,16},{24,152},{152,24... | collective-permute-start | bytes 2359304 | tf_op jit(solution)/shard_map/ppermute | solution.py:18
  178.0 20.5 %collective-permute-start.3 = (f32[2,96,2,512]{3,1,2,0:T(8,128)S(1)}, f32[2,96,2,512]{3,1,2,0:T(8,128)S(1)}, u32[]{:S(2)}, u32[]{:S(2)}) collective-permute-start(f32[2,96,2,512]{3,1,2,0:T(8,128)S(1)} %maximum_select_fusion.1), channel_id=1, source_target_pairs={{0,64},{64,0},{8,72},{72,8},{16,80},{80,16},{24,88},{88,24},{32,96... | collective-permute-start | bytes 2359304 | tf_op jit(solution)/shard_map/ppermute | solution.py:18
  198.9 21.2 %collective-permute-start.4 = (f32[2,96,2,512]{3,1,2,0:T(8,128)S(1)}, f32[2,96,2,512]{3,1,2,0:T(8,128)S(1)}, u32[]{:S(2)}, u32[]{:S(2)}) collective-permute-start(f32[2,96,2,512]{3,1,2,0:T(8,128)S(1)} %maximum_select_fusion.2), channel_id=1, source_target_pairs={{0,32},{32,0},{8,40},{40,8},{16,48},{48,16},{24,56},{56,24},{64,96... | collective-permute-start | bytes 2359304 | tf_op jit(solution)/shard_map/ppermute | solution.py:18
  220.5 18.8 %collective-permute-start.5 = (f32[2,96,2,512]{3,1,2,0:T(8,128)S(1)}, f32[2,96,2,512]{3,1,2,0:T(8,128)S(1)}, u32[]{:S(2)}, u32[]{:S(2)}) collective-permute-start(f32[2,96,2,512]{3,1,2,0:T(8,128)S(1)} %maximum_select_fusion.3), channel_id=1, source_target_pairs={{0,16},{16,0},{8,24},{24,8},{32,48},{48,32},{40,56},{56,40},{64,80... | collective-permute-start | bytes 2359304 | tf_op jit(solution)/shard_map/ppermute | solution.py:18
  239.8 8.3 %collective-permute-start.6 = (f32[2,96,2,512]{3,1,2,0:T(8,128)S(1)}, f32[2,96,2,512]{3,1,2,0:T(8,128)S(1)}, u32[]{:S(2)}, u32[]{:S(2)}) collective-permute-start(f32[2,96,2,512]{3,1,2,0:T(8,128)S(1)} %maximum_select_fusion.4), channel_id=1, source_target_pairs={{0,8},{8,0},{16,24},{24,16},{32,40},{40,32},{48,56},{56,48},{64,72... | collective-permute-start | bytes 2359304 | tf_op jit(solution)/shard_map/ppermute | solution.py:18
  257.7 9.6 %collective-permute-start.8 = (f32[2,32,2,512]{3,1,2,0:T(8,128)S(1)}, f32[2,32,2,512]{3,1,2,0:T(8,128)S(1)}, u32[]{:S(2)}, u32[]{:S(2)}) collective-permute-start(f32[2,32,2,512]{3,1,2,0:T(8,128)S(1)} %fusion.34), channel_id=1, source_target_pairs={{0,16},{16,0},{8,24},{24,8},{32,48},{48,32},{40,56},{56,40},{64,80... | collective-permute-start | bytes 786440 | tf_op jit(solution)/shard_map/ppermute | solution.py:18
  267.6 10.3 %collective-permute-start.9 = (f32[2,32,2,512]{3,1,2,0:T(8,128)S(1)}, f32[2,32,2,512]{3,1,2,0:T(8,128)S(1)}, u32[]{:S(2)}, u32[]{:S(2)}) collective-permute-start(f32[2,32,2,512]{3,1,2,0:T(8,128)S(1)} %fusion.35), channel_id=1, source_target_pairs={{0,32},{32,0},{8,40},{40,8},{16,48},{48,16},{24,56},{56,24},{64,96... | collective-permute-start | bytes 786440 | tf_op jit(solution)/shard_map/ppermute | solution.py:18
  278.0 7.9 %collective-permute-start.10 = (f32[2,32,2,512]{3,1,2,0:T(8,128)S(1)}, f32[2,32,2,512]{3,1,2,0:T(8,128)S(1)}, u32[]{:S(2)}, u32[]{:S(2)}) collective-permute-start(f32[2,32,2,512]{3,1,2,0:T(8,128)S(1)} %fusion.36), channel_id=1, source_target_pairs={{0,64},{64,0},{8,72},{72,8},{16,80},{80,16},{24,88},{88,24},{32,96... | collective-permute-start | bytes 786440 | tf_op jit(solution)/shard_map/ppermute | solution.py:18
  286.1 16.3 %collective-permute-start.11 = (f32[2,32,2,512]{3,1,2,0:T(8,128)S(1)}, f32[2,32,2,512]{3,1,2,0:T(8,128)S(1)}, u32[]{:S(2)}, u32[]{:S(2)}) collective-permute-start(f32[2,32,2,512]{3,1,2,0:T(8,128)S(1)} %fusion.37), channel_id=1, source_target_pairs={{0,128},{128,0},{8,136},{136,8},{16,144},{144,16},{24,152},{152,24... | collective-permute-start | bytes 786440 | tf_op jit(solution)/shard_map/ppermute | solution.py:18
  302.5 19.5 %collective-permute-start.12 = (f32[2,32,2,512]{3,1,2,0:T(8,128)S(1)}, f32[2,32,2,512]{3,1,2,0:T(8,128)S(1)}, u32[]{:S(2)}, u32[]{:S(2)}) collective-permute-start(f32[2,32,2,512]{3,1,2,0:T(8,128)S(1)} %fusion.38), channel_id=1, source_target_pairs={{0,256},{256,0},{8,264},{264,8},{16,272},{272,16},{24,280},{280,24... | collective-permute-start | bytes 786440 | tf_op jit(solution)/shard_map/ppermute | solution.py:18
  322.3 13.1 %collective-permute-start.13 = (f32[2,32,2,512]{3,1,2,0:T(8,128)S(1)}, f32[2,32,2,512]{3,1,2,0:T(8,128)S(1)}, u32[]{:S(2)}, u32[]{:S(2)}) collective-permute-start(f32[2,32,2,512]{3,1,2,0:T(8,128)S(1)} %pad_maximum_fusion.12), channel_id=1, source_target_pairs={{0,256},{256,0},{8,264},{264,8},{16,272},{272,16},{24,280},{280,24... | collective-permute-start | bytes 786440 | tf_op jit(solution)/shard_map/ppermute | solution.py:18
  335.5 15.7 %collective-permute-start.14 = (f32[2,32,2,512]{3,1,2,0:T(8,128)S(1)}, f32[2,32,2,512]{3,1,2,0:T(8,128)S(1)}, u32[]{:S(2)}, u32[]{:S(2)}) collective-permute-start(f32[2,32,2,512]{3,1,2,0:T(8,128)S(1)} %maximum_select_fusion.6), channel_id=1, source_target_pairs={{0,128},{128,0},{8,136},{136,8},{16,144},{144,16},{24,152},{152,24... | collective-permute-start | bytes 786440 | tf_op jit(solution)/shard_map/ppermute | solution.py:18
  351.4 8.3 %collective-permute-start.15 = (f32[2,32,2,512]{3,1,2,0:T(8,128)S(1)}, f32[2,32,2,512]{3,1,2,0:T(8,128)S(1)}, u32[]{:S(2)}, u32[]{:S(2)}) collective-permute-start(f32[2,32,2,512]{3,1,2,0:T(8,128)S(1)} %maximum_select_fusion.7), channel_id=1, source_target_pairs={{0,64},{64,0},{8,72},{72,8},{16,80},{80,16},{24,88},{88,24},{32,96... | collective-permute-start | bytes 786440 | tf_op jit(solution)/shard_map/ppermute | solution.py:18
  359.8 8.9 %collective-permute-start.16 = (f32[2,32,2,512]{3,1,2,0:T(8,128)S(1)}, f32[2,32,2,512]{3,1,2,0:T(8,128)S(1)}, u32[]{:S(2)}, u32[]{:S(2)}) collective-permute-start(f32[2,32,2,512]{3,1,2,0:T(8,128)S(1)} %maximum_select_fusion.8), channel_id=1, source_target_pairs={{0,32},{32,0},{8,40},{40,8},{16,48},{48,16},{24,56},{56,24},{64,96... | collective-permute-start | bytes 786440 | tf_op jit(solution)/shard_map/ppermute | solution.py:18
  368.9 7.1 %collective-permute-start.17 = (f32[2,32,2,512]{3,1,2,0:T(8,128)S(1)}, f32[2,32,2,512]{3,1,2,0:T(8,128)S(1)}, u32[]{:S(2)}, u32[]{:S(2)}) collective-permute-start(f32[2,32,2,512]{3,1,2,0:T(8,128)S(1)} %maximum_select_fusion.9), channel_id=1, source_target_pairs={{0,16},{16,0},{8,24},{24,8},{32,48},{48,32},{40,56},{56,40},{64,80... | collective-permute-start | bytes 786440 | tf_op jit(solution)/shard_map/ppermute | solution.py:18
  376.1 7.4 %collective-permute-start.18 = (f32[2,32,2,512]{3,1,2,0:T(8,128)S(1)}, f32[2,32,2,512]{3,1,2,0:T(8,128)S(1)}, u32[]{:S(2)}, u32[]{:S(2)}) collective-permute-start(f32[2,32,2,512]{3,1,2,0:T(8,128)S(1)} %maximum_select_fusion.10), channel_id=1, source_target_pairs={{0,8},{8,0},{16,24},{24,16},{32,40},{40,32},{48,56},{56,48},{64,72... | collective-permute-start | bytes 786440 | tf_op jit(solution)/shard_map/ppermute | solution.py:18
  391.1 9.4 %collective-permute-start.20 = (f32[2,32,2,512]{3,1,2,0:T(8,128)S(1)}, f32[2,32,2,512]{3,1,2,0:T(8,128)S(1)}, u32[]{:S(2)}, u32[]{:S(2)}) collective-permute-start(f32[2,32,2,512]{3,1,2,0:T(8,128)S(1)} %fusion.40), channel_id=1, source_target_pairs={{0,16},{16,0},{8,24},{24,8},{32,48},{48,32},{40,56},{56,40},{64,80... | collective-permute-start | bytes 786440 | tf_op jit(solution)/shard_map/ppermute | solution.py:18
  400.7 10.0 %collective-permute-start.21 = (f32[2,32,2,512]{3,1,2,0:T(8,128)S(1)}, f32[2,32,2,512]{3,1,2,0:T(8,128)S(1)}, u32[]{:S(2)}, u32[]{:S(2)}) collective-permute-start(f32[2,32,2,512]{3,1,2,0:T(8,128)S(1)} %fusion.41), channel_id=1, source_target_pairs={{0,32},{32,0},{8,40},{40,8},{16,48},{48,16},{24,56},{56,24},{64,96... | collective-permute-start | bytes 786440 | tf_op jit(solution)/shard_map/ppermute | solution.py:18
  410.9 7.7 %collective-permute-start.22 = (f32[2,32,2,512]{3,1,2,0:T(8,128)S(1)}, f32[2,32,2,512]{3,1,2,0:T(8,128)S(1)}, u32[]{:S(2)}, u32[]{:S(2)}) collective-permute-start(f32[2,32,2,512]{3,1,2,0:T(8,128)S(1)} %fusion.42), channel_id=1, source_target_pairs={{0,64},{64,0},{8,72},{72,8},{16,80},{80,16},{24,88},{88,24},{32,96... | collective-permute-start | bytes 786440 | tf_op jit(solution)/shard_map/ppermute | solution.py:18
  418.7 16.1 %collective-permute-start.23 = (f32[2,32,2,512]{3,1,2,0:T(8,128)S(1)}, f32[2,32,2,512]{3,1,2,0:T(8,128)S(1)}, u32[]{:S(2)}, u32[]{:S(2)}) collective-permute-start(f32[2,32,2,512]{3,1,2,0:T(8,128)S(1)} %fusion.43), channel_id=1, source_target_pairs={{0,128},{128,0},{8,136},{136,8},{16,144},{144,16},{24,152},{152,24... | collective-permute-start | bytes 786440 | tf_op jit(solution)/shard_map/ppermute | solution.py:18
  434.9 15.6 %collective-permute-start.24 = (f32[2,32,2,512]{3,1,2,0:T(8,128)S(1)}, f32[2,32,2,512]{3,1,2,0:T(8,128)S(1)}, u32[]{:S(2)}, u32[]{:S(2)}) collective-permute-start(f32[2,32,2,512]{3,1,2,0:T(8,128)S(1)} %fusion.44), channel_id=1, source_target_pairs={{0,256},{256,0},{8,264},{264,8},{16,272},{272,16},{24,280},{280,24... | collective-permute-start | bytes 786440 | tf_op jit(solution)/shard_map/ppermute | solution.py:18
  (8 other events, 204.8 us)
Sparse Core Ops, SparseCore 0:
  452.1 34.0 reduce-scatter.3
where the time goes:
time: 500 us; the launch traced here: 494 us
  waiting for transfers between devices  268 us (54%)
  starting transfers between devices  115 us (23%)
  blocking collectives  62.7 us (13%)
  between operations  16.3 us (3%)
  other arithmetic  16.1 us (3%)
  matrix products  11.1 us (2%)
  local copies, waits for them, and re-layouts  5.54 us (1%)
    ppermute x24, waiting for transfers between devices, swapped(): return lax.ppermute(block, axis, route)  233 us
    ppermute x24, starting transfers between devices, swapped(): return lax.ppermute(block, axis, route)  101 us
    unnamed x1, blocking collectives  62.7 us
    reduce_scatter x1, waiting for transfers between devices, local(): lax.psum_scatter(jnp.einsum('io,it->ot', columns, mixed, preferred_elemen...  34.2 us
    ppermute x1, starting transfers between devices, passed_along(): return lax.ppermute(shard, axis, pairs)  14.3 us
  transfers between devices with their start and end apart: 26, of which 25 were waited for; matrix products, arithmetic and copies ran while one was open for 1% of the time, Pallas kernels for 0%

commit v1 on v0

v1 whole, which is shorter than its diff:
```python
import functools

import jax
import jax.numpy as jnp
import numpy as np
from jax import lax
from jax.experimental import pallas as pl
from jax.experimental.pallas import tpu as pltpu
from jax.sharding import PartitionSpec as P

bf16 = jnp.bfloat16
f32 = jnp.float32

ROWS = 128
COLS = 256
TOTAL = ROWS * COLS
PLANE = 32
GROUPS = 8
BLOCK = 512


def split(values):
    high = values.astype(bf16)
    return high, (values - high.astype(f32)).astype(bf16)


def halves(table):
    table = np.asarray(table, np.float32)
    high = table.astype(jnp.bfloat16)
    low = (table - high.astype(np.float32)).astype(jnp.bfloat16)
    return high, low


@functools.cache
def tables():
    row = (4 * np.arange(PLANE)[None, :] + np.arange(4)[:, None]).reshape(-1).astype(np.float64)
    freq = 4.0 * np.arange(ROWS) + 1.0
    angle = 2.0 * np.pi * ((freq[:, None] * row[None, :]) % (4 * ROWS)) / (4 * ROWS)
    first = np.concatenate([np.cos(angle), -np.sin(angle)], axis=0)
    column = np.arange(COLS, dtype=np.float64)
    turn = 2.0 * np.pi * ((freq[:, None] * column[None, :]) % (4 * TOTAL)) / (4 * TOTAL)
    twiddle = np.stack([np.cos(turn), -np.sin(turn)]).astype(np.float32)
    inner = 2.0 * np.pi * ((column[:, None] * column[None, :]) % COLS) / COLS
    second = np.concatenate([np.cos(inner), np.sin(inner)], axis=1)
    return {
        "first": np.stack(halves(first)),
        "last": np.stack(halves(first.T / TOTAL)),
        "twiddle": twiddle,
        "second": np.stack(halves(second)),
    }


def interleave(outer, inner):
    table = np.zeros((outer * inner, outer * inner), np.float32)
    for a in range(outer):
        for b in range(inner):
            table[a * inner + b, b * outer + a] = 1.0
    return table.astype(jnp.bfloat16)


def mm(left, right):
    return jnp.dot(left, right, preferred_element_type=f32)


def left_product(table, values):
    high, low = split(values)
    return mm(table[0], high) + mm(table[0], low) + mm(table[1], high)


def right_product(values, table):
    high, low = split(values)
    return mm(high, table[0]) + mm(low, table[0]) + mm(high, table[1])


def pack_kernel(x_ref, proj_ref, out_w_ref, o_ref):
    x = x_ref[...]
    weights = [proj_ref[g].astype(f32) for g in range(3)] + [out_w_ref[...].astype(f32)]
    lane = lax.broadcasted_iota(jnp.int32, (32, 128), 1) // 32
    for z in range(GROUPS):
        tile, offset = z // 4, z % 4
        picked = None
        for g in range(4):
            piece = weights[g][:, 128 * tile : 128 * tile + 128]
            by = (32 * (g - offset)) % 128
            if by:
                piece = pltpu.roll(piece, by, 1)
            picked = piece if picked is None else jnp.where(lane == g, piece, picked)
        o_ref[z, :, 0:BLOCK] = x
        o_ref[z, :, BLOCK : BLOCK + 128] = picked.astype(bf16)


def project_kernel(r_ref, filters_ref, perm_ref, o_ref):
    x = r_ref[:, 0:BLOCK]
    weights = r_ref[:, BLOCK : BLOCK + 128]
    projected = lax.dot_general(
        weights, x, (((0,), (0,)), ((), ())), preferred_element_type=f32
    ).astype(bf16)
    filters = jnp.concatenate([filters_ref[0], filters_ref[1]], axis=0)
    high, low = split(filters)
    stacked = jnp.concatenate([projected, high, low], axis=0)
    o_ref[...] = mm(perm_ref[...], stacked).astype(bf16)


def forward(signals, first, twiddle, second):
    count = len(signals)
    stage = left_product(first, jnp.concatenate(signals, axis=1))
    rows = []
    for s in range(count):
        real = stage[:ROWS, COLS * s : COLS * (s + 1)]
        imag = stage[ROWS:, COLS * s : COLS * (s + 1)]
        rows.append(real * twiddle[0] - imag * twiddle[1])
        rows.append(real * twiddle[1] + imag * twiddle[0])
    product = right_product(jnp.concatenate(rows, axis=0), second)
    spectra = []
    for s in range(count):
        real = product[2 * ROWS * s : 2 * ROWS * s + ROWS]
        imag = product[2 * ROWS * s + ROWS : 2 * ROWS * (s + 1)]
        spectra.append((real[:, :COLS] + imag[:, COLS:], imag[:, :COLS] - real[:, COLS:]))
    return spectra


def inverse(spectrum, last, twiddle, second):
    product = right_product(jnp.concatenate(spectrum, axis=0), second)
    real = product[:ROWS, :COLS] - product[ROWS:, COLS:]
    imag = product[ROWS:, :COLS] + product[:ROWS, COLS:]
    turned_real = real * twiddle[0] + imag * twiddle[1]
    turned_imag = imag * twiddle[0] - real * twiddle[1]
    return left_product(last, jnp.concatenate([turned_real, turned_imag], axis=0))


def times(left, right):
    return (left[0] * right[0] - left[1] * right[1], left[0] * right[1] + left[1] * right[0])


def short_filter(blocks, taps, group):
    lane = lax.broadcasted_iota(jnp.int32, (PLANE, COLS), 1)
    chip = lax.broadcasted_iota(jnp.int32, (PLANE, COLS), 0)
    shifted = []
    for by in (1, 2):
        rolled = [pltpu.roll(block, by, 1) for block in blocks]
        before = jnp.where(chip == 0, 0.0, pltpu.roll(rolled[3], 1, 0))
        edges = [before, rolled[0], rolled[1], rolled[2]]
        shifted.append([jnp.where(lane < by, edges[q], rolled[q]) for q in range(4)])
    tap = [taps[group : group + 1, j : j + 1] for j in range(3)]
    return [
        tap[0] * blocks[q] + tap[1] * shifted[0][q] + tap[2] * shifted[1][q] for q in range(4)
    ]


def convolve(core, mine, other, taps, gains, perm, first, last, own_last, twiddle, second, spread):
    parts = [
        mm(perm, jnp.where(core == 0, mine, other)),
        mm(perm, jnp.where(core == 0, other, mine)),
    ]

    def classes(slot):
        return [
            parts[q // 2][PLANE * slot : PLANE * (slot + 1), COLS * (q % 2) : COLS * (q % 2 + 1)]
            for q in range(4)
        ]

    groups = [jnp.concatenate(short_filter(classes(g), taps, g), axis=0) for g in range(3)]
    responses = [
        jnp.concatenate(classes(4 + f), axis=0) + jnp.concatenate(classes(6 + f), axis=0)
        for f in range(2)
    ]
    values, first_gate, second_gate = groups
    value_spectrum, first_spectrum, second_spectrum = forward(
        [values] + responses, first, twiddle, second
    )
    convolved = inverse(times(value_spectrum, first_spectrum), last, twiddle, second)
    gated = first_gate * (convolved + gains[:, 0:1] * values)
    (gated_spectrum,) = forward([gated], first, twiddle, second)
    own = inverse(times(gated_spectrum, second_spectrum), own_last, twiddle, second)
    half = ROWS // 2
    own_gated = jnp.where(core == 0, gated[:half], gated[half:])
    own_gate = jnp.where(core == 0, second_gate[:half], second_gate[half:])
    mixed = (own_gate * (own + gains[:, 1:2] * own_gated)).astype(bf16)
    lanes = jnp.concatenate(
        [
            mixed[PLANE * (j // 2) : PLANE * (j // 2 + 1), 128 * (j % 2) : 128 * (j % 2 + 1)]
            for j in range(4)
        ],
        axis=0,
    )
    return mm(spread, lanes).astype(bf16)


def convolve_kernel(
    mine_ref, other_ref, taps_ref, gains_ref, perm_ref, first_ref, last_ref, twiddle_ref,
    second_ref, spread_ref, o_ref,
):
    device = lax.axis_index("seq")
    core = device % 2
    channel = device // 2
    half = ROWS // 2
    out = convolve(
        core,
        mine_ref[...],
        other_ref[...],
        taps_ref[channel],
        gains_ref[pl.ds(channel, 1), :],
        perm_ref[...],
        first_ref,
        last_ref,
        [last_ref[i, pl.ds(pl.multiple_of(half * core, half), half), :] for i in range(2)],
        twiddle_ref,
        second_ref,
        spread_ref[...],
    )
    for z in range(GROUPS):
        o_ref[z] = out


def output_kernel(r_ref, weights_ref, o_ref, scratch):
    scratch[...] = r_ref[...].astype(f32)
    mixed = jnp.concatenate(
        [scratch[pl.ds(j, 256, stride=4), :].astype(bf16) for j in range(4)], axis=1
    )
    weights = weights_ref[:, 96:128]
    o_ref[...] = lax.dot_general(
        weights, mixed, (((0,), (0,)), ((), ())), preferred_element_type=f32
    ).astype(bf16)


def local(inputs, proj_weight, short_taps, skip_gain, filters, out_weight):
    table = tables()
    packed = pl.pallas_call(
        pack_kernel,
        out_shape=jax.ShapeDtypeStruct((GROUPS, 32, BLOCK + 128), bf16),
        name="pack",
    )(inputs, proj_weight, out_weight)
    gathered = lax.all_to_all(packed, "ch", 0, 0, tiled=True).reshape(256, BLOCK + 128)

    perm = interleave(PLANE, 8)
    sent = pl.pallas_call(
        project_kernel,
        out_shape=jax.ShapeDtypeStruct((256, BLOCK), bf16),
        name="project",
    )(gathered, filters, perm)
    same_core = [[2 * c + k for c in range(PLANE)] for k in range(2)]
    mine = lax.all_to_all(
        sent.reshape(PLANE, 8, BLOCK), "seq", 0, 0, tiled=True, axis_index_groups=same_core
    ).reshape(256, BLOCK)
    other = lax.ppermute(mine, "seq", [(i, i ^ 1) for i in range(2 * PLANE)])

    mixed = pl.pallas_call(
        convolve_kernel,
        out_shape=jax.ShapeDtypeStruct((GROUPS, 128, 128), bf16),
        name="convolve",
    )(
        mine,
        other,
        short_taps,
        skip_gain,
        np.ascontiguousarray(perm.T),
        table["first"],
        table["last"],
        table["twiddle"],
        table["second"],
        interleave(PLANE, 4),
    )
    everyone = [
        [(2 * c + k) * GROUPS + z for z in range(GROUPS) for c in range(PLANE)] for k in range(2)
    ]
    arrived = lax.all_to_all(
        mixed.reshape(256, 4, 128),
        ("seq", "ch"),
        0,
        0,
        tiled=True,
        axis_index_groups=everyone,
    ).reshape(1024, 128)
    return pl.pallas_call(
        output_kernel,
        out_shape=jax.ShapeDtypeStruct((32, BLOCK), bf16),
        in_specs=[
            pl.BlockSpec((1024, 128), lambda i: (0, 0)),
            pl.BlockSpec((256, 128), lambda i: (0, 4)),
        ],
        out_specs=pl.BlockSpec((32, BLOCK), lambda i: (0, 0)),
        grid=(1,),
        scratch_shapes=[pltpu.VMEM((1024, 128), f32)],
        name="output",
    )(arrived, gathered)


def solution(mesh):
    in_specs = (
        P("ch", "seq"),
        P(None, "ch", None),
        P("ch", None, None),
        P("ch", None),
        P(None, "ch", "seq"),
        P("ch", None),
    )
    return jax.shard_map(
        local, mesh=mesh, in_specs=in_specs, out_specs=P("ch", "seq"), check_vma=False
    )
```

time: 500 us -> 88.2 us (0.18); the launches traced: 494 us -> 87.7 us
  waiting for transfers between devices: 268 us -> 0.01 us
  starting transfers between devices: 115 us -> 5.95 us
  between operations: 16.3 us -> 0.03 us
  other arithmetic: 16.1 us -> 0 us
  Pallas kernels: 0 us -> 12.4 us
  matrix products: 11.1 us -> 0 us
    ppermute x25 -> x1, waiting for transfers between devices: 233 us -> 0.01 us  [local(): other = lax.ppermute(mine, 'seq', [(i, i ^ 1) for i in range(2 * PLANE)])]
    ppermute x25 -> x1, starting transfers between devices: 115 us -> 5.95 us  [local(): other = lax.ppermute(mine, 'seq', [(i, i ^ 1) for i in range(2 * PLANE)])]
    all_to_all x0 -> x3, blocking collectives: none -> 67.2 us  [the longest x1 24.4 us: local(): lax.all_to_all(mixed.reshape(256, 4, 128), ('seq', 'ch'), 0, 0, tiled=Tru...]
    unnamed x1 -> x0, blocking collectives: 62.7 us -> none
    reduce_scatter x1 -> x0, waiting for transfers between devices: 34.2 us -> none  [local(): lax.psum_scatter(jnp.einsum('io,it->ot', columns, mixed, preferred_elemen...]
    pallas_call x0 -> x4, Pallas kernels: none -> 12.4 us  [the longest x1 6.69 us: local(): pl.pallas_call(convolve_kernel, out_shape=jax.ShapeDtypeStruct((GROUPS, 1...]
    dot_general x18 -> x0, matrix products: 11.1 us -> none  [the longest x16 8.49 us: local_dft(): products = jnp.einsum('xrem,ymd->xyred', spectrum, table, precision=highest)]
    select_n x24 -> x0, other arithmetic: 5.56 us -> none  [the longest x12 4.22 us: forward(): state = jnp.where(upper, turned, state + partner)]
  transfers between devices with their start and end apart: 26 -> 1, of which waited for: 25 -> 0; matrix products, arithmetic and copies ran while one was open for 1% -> 2% of each run, Pallas kernels for 0% -> 0%
where the time goes in v1:
time: 88.2 us; the launch traced here: 87.7 us
  blocking collectives  67.2 us (76%)
  Pallas kernels  12.4 us (14%)
  starting transfers between devices  5.95 us (7%)
  local copies, waits for them, and re-layouts  2.13 us (2%)
    all_to_all x1, blocking collectives, local(): lax.all_to_all(mixed.reshape(256, 4, 128), ('seq', 'ch'), 0, 0, tiled=Tru...  24.4 us
    all_to_all x1, blocking collectives, local(): lax.all_to_all(packed, 'ch', 0, 0, tiled=True).reshape(256, BLOCK + 128)  22.7 us
    all_to_all x1, blocking collectives, local(): lax.all_to_all(sent.reshape(PLANE, 8, BLOCK), 'seq', 0, 0, tiled=True, ax...  20.2 us
    pallas_call x1, Pallas kernels, local(): pl.pallas_call(convolve_kernel, out_shape=jax.ShapeDtypeStruct((GROUPS, 1...  6.69 us
    ppermute x1, starting transfers between devices, local(): other = lax.ppermute(mine, 'seq', [(i, i ^ 1) for i in range(2 * PLANE)])  5.95 us
    pallas_call x1, Pallas kernels, local(): pl.pallas_call(project_kernel, out_shape=jax.ShapeDtypeStruct((256, BLOCK...  2.2 us
    unnamed x10, local copies, waits for them, and re-layouts  2.13 us
    pallas_call x1, Pallas kernels, local(): pl.pallas_call(output_kernel, out_shape=jax.ShapeDtypeStruct((32, BLOCK),...  1.81 us
  transfers between devices with their start and end apart: 1, of which 0 were waited for; matrix products, arithmetic and copies ran while one was open for 2% of the time, Pallas kernels for 0%

profile of v1, /device:TPU:1, one launch (start us, length us, event | category | flops | bytes accessed | tf_op | source)
XLA Modules:
  0.0 87.7 jit_solution(4340175288687436599)
XLA Ops:
  0.0 1.7 %pack.1 = bf16[8,32,640]{2,1,0:T(8,128)(2,1)} custom-call(bf16[32,512]{1,0:T(8,128)(2,1)} %x_ref.1, bf16[3,32,256]{2,1,0:T(8,128)(2,1)} %proj_ref.1, bf16[32,256]{1,0:T(8,128)(2,1)} %out_w_ref.1), custom_call_target="tpu_custom_call" | custom-call | tf_op jit(solution)/shard_map/pack/pallas_call | solution.py:228
  1.7 22.7 %all_to_all.15 = bf16[8,32,640]{2,1,0:T(8,128)(2,1)} all-to-all(bf16[8,32,640]{2,1,0:T(8,128)(2,1)} %pack.1), channel_id=1, replica_groups=mesh['seq'=64,'ch'=8] {'ch'}, dimensions={0} | all-to-all | bytes 655360 | tf_op jit(solution)/shard_map/all_to_all | solution.py:233
  24.4 2.2 %project.1 = bf16[256,512]{1,0:T(8,128)(2,1)} custom-call(bf16[256,640]{1,0:T(8,128)(2,1)} %bitcast.5, f32[2,32,512]{2,1,0:T(8,128)} %filters_ref.1, bf16[256,256]{1,0:T(8,128)(2,1)} %constant.14.clone.perm_ref), custom_call_target="tpu_custom_call" | custom-call | tf_op jit(solution)/shard_map/project/pallas_call | solution.py:236
  26.6 20.2 %all_to_all.16 = bf16[32,8,512]{2,1,0:T(8,128)(2,1)S(1)} all-to-all(bf16[32,8,512]{2,1,0:T(8,128)(2,1)} %bitcast.8), channel_id=1, replica_groups={{0,16,32,48,64,80,96,112,128,144,160,176,192,208,224,240,256,272,288,30..., dimensions={0} | all-to-all | bytes 524288 | tf_op jit(solution)/shard_map/all_to_all | solution.py:242
  46.7 0.0 copy-start
  46.7 0.0 copy-start.3
  46.7 0.0 copy-start.2
  46.7 6.0 %collective-permute-start = (bf16[256,512]{1,0:T(8,128)(2,1)S(1)}, bf16[256,512]{1,0:T(8,128)(2,1)S(1)}, u32[]{:S(2)}, u32[]{:S(2)}) collective-permute-start(bf16[256,512]{1,0:T(8,128)(2,1)S(1)} %bitcast.9), channel_id=1, source_target_pairs={{0,8},{8,0},{16,24},{24,16},{32,40},{40,32},{48,56},{56,48},{64,72... | collective-permute-start | bytes 786440 | tf_op jit(solution)/shard_map/ppermute | solution.py:245
  52.7 0.0 copy-done.3
  52.7 0.7 copy.15.gains_ref
  53.4 0.0 copy-done.2
  53.4 0.7 copy.14.taps_ref
  54.1 0.0 collective-permute-done.other_ref
  54.1 0.0 copy-done
  54.1 0.0 copy-start.1
  54.1 0.7 copy-done.1
  54.8 6.7 %convolve.1 = bf16[8,128,128]{2,1,0:T(8,128)(2,1)} custom-call(bf16[256,512]{1,0:T(8,128)(2,1)} %bitcast.10, bf16[256,512]{1,0:T(8,128)(2,1)} %copy-done.1, f32[32,3,3]{2,1,0:T(4,128)} %copy.14.taps_ref, f32[32,2]{1,0:T(8,128)} %copy.15.gains_ref, bf16[256,256]{1,0:T(8,128)(2,1)} %constant.15.clone.perm_ref, bf16[2,256,128]{2,1,0:T(8,128)(2,1)} %constant.16.clone.first_ref, ...), custom_call_target="tpu_custom_call" | custom-call | tf_op jit(solution)/shard_map/convolve/pallas_call | solution.py:247
  61.5 24.4 %all_to_all.17 = bf16[256,4,128]{2,1,0:T(4,128)(2,1)} all-to-all(bf16[256,4,128]{2,1,0:T(4,128)(2,1)} %bitcast.11), channel_id=1, replica_groups={{0,16,32,48,64,80,96,112,128,144,160,176,192,208,224,240,256,272,288,30..., dimensions={0} | all-to-all | bytes 524288 | tf_op jit(solution)/shard_map/all_to_all | solution.py:266
  85.9 1.8 %output.1 = bf16[32,512]{1,0:T(8,128)(2,1)} custom-call(bf16[1024,128]{1,0:T(8,128)(2,1)} %bitcast.7, bf16[256,640]{1,0:T(8,128)(2,1)} %bitcast.6), custom_call_target="tpu_custom_call" | custom-call | tf_op jit(solution)/shard_map/output/pallas_call | solution.py:274
Async XLA Ops:
  46.7 7.4 %copy-start = (bf16[32,8,512]{2,1,0:T(8,128)(2,1)}, bf16[32,8,512]{2,1,0:T(8,128)(2,1)S(1)}, u32[]{:S(2)}) copy-start(bf16[32,8,512]{2,1,0:T(8,128)(2,1)S(1)} %all_to_all.16) | copy-start | bytes 786436
  46.7 6.0 %copy-start.3 = (f32[32,2]{0,1:T(2,128)S(1)}, f32[32,2]{0,1:T(2,128)}, u32[]{:S(2)}) copy-start(f32[32,2]{0,1:T(2,128)} %param.16) | copy-start | bytes 772
  46.7 6.7 %copy-start.2 = (f32[32,3,3]{0,2,1:T(4,128)S(1)}, f32[32,3,3]{0,2,1:T(4,128)}, u32[]{:S(2)}) copy-start(f32[32,3,3]{0,2,1:T(4,128)} %param.15) | copy-start | bytes 3460
  46.7 7.4 %collective-permute-start = (bf16[256,512]{1,0:T(8,128)(2,1)S(1)}, bf16[256,512]{1,0:T(8,128)(2,1)S(1)}, u32[]{:S(2)}, u32[]{:S(2)}) collective-permute-start(bf16[256,512]{1,0:T(8,128)(2,1)S(1)} %bitcast.9), channel_id=1, source_target_pairs={{0,8},{8,0},{16,24},{24,16},{32,40},{40,32},{48,56},{56,48},{64,72... | collective-permute-start | bytes 786440 | tf_op jit(solution)/shard_map/ppermute | solution.py:245
  54.1 0.7 copy-start.1

commit v2 on v1

v2 whole, which is shorter than its diff:
```python
import functools

import jax
import jax.numpy as jnp
import numpy as np
from jax import lax
from jax.experimental import pallas as pl
from jax.experimental.pallas import tpu as pltpu
from jax.sharding import PartitionSpec as P

bf16 = jnp.bfloat16
f32 = jnp.float32

ROWS = 128
COLS = 256
TOTAL = ROWS * COLS
PLANE = 32
GROUPS = 8
BLOCK = 512
CHUNK = 20


def split(values):
    high = values.astype(bf16)
    return high, (values - high.astype(f32)).astype(bf16)


def halves(table):
    table = np.asarray(table, np.float32)
    high = table.astype(jnp.bfloat16)
    low = (table - high.astype(np.float32)).astype(jnp.bfloat16)
    return high, low


@functools.cache
def tables():
    row = (4 * np.arange(PLANE)[None, :] + np.arange(4)[:, None]).reshape(-1).astype(np.float64)
    freq = 4.0 * np.arange(ROWS) + 1.0
    angle = 2.0 * np.pi * ((freq[:, None] * row[None, :]) % (4 * ROWS)) / (4 * ROWS)
    first = np.concatenate([np.cos(angle), -np.sin(angle)], axis=0)
    column = np.arange(COLS, dtype=np.float64)
    turn = 2.0 * np.pi * ((freq[:, None] * column[None, :]) % (4 * TOTAL)) / (4 * TOTAL)
    inner = 2.0 * np.pi * ((column[:, None] * column[None, :]) % COLS) / COLS
    cosine, sine = np.cos(inner), np.sin(inner)
    high, low = halves(first)
    return {
        "first": np.stack(
            [np.concatenate([high, high], axis=1), np.concatenate([high, low], axis=1)]
        ),
        "last": np.stack(halves(first.T / TOTAL)),
        "twiddle": np.stack([np.cos(turn), -np.sin(turn)]).astype(np.float32),
        "second": np.stack([np.stack(halves(t)) for t in (cosine, cosine + sine, cosine - sine)]),
    }


def mm(left, right):
    return jnp.dot(left, right, preferred_element_type=f32)


def left_product(table, values):
    high, low = split(values)
    return mm(table[0], high) + mm(table[0], low) + mm(table[1], high)


def right_product(values, table):
    high, low = split(values)
    return mm(high, table[0]) + mm(low, table[0]) + mm(high, table[1])


def pack_kernel(x_hbm, proj_hbm, out_w_hbm, o_ref, x_ref, proj_ref, out_w_ref, sems):
    copies = [
        pltpu.make_async_copy(proj_hbm, proj_ref, sems.at[0]),
        pltpu.make_async_copy(out_w_hbm, out_w_ref, sems.at[1]),
        pltpu.make_async_copy(x_hbm, x_ref, sems.at[2]),
    ]
    for copy in copies:
        copy.start()
    copies[0].wait()
    copies[1].wait()
    weights = [proj_ref[g].astype(f32) for g in range(3)] + [out_w_ref[...].astype(f32)]
    lane = lax.broadcasted_iota(jnp.int32, (32, 128), 1) // 32
    for z in range(GROUPS):
        tile, offset = z // 4, z % 4
        picked = None
        for g in range(4):
            piece = weights[g][:, 128 * tile : 128 * tile + 128]
            by = (32 * (g - offset)) % 128
            if by:
                piece = pltpu.roll(piece, by, 1)
            picked = piece if picked is None else jnp.where(lane == g, piece, picked)
        o_ref[z, :, BLOCK : BLOCK + 128] = picked.astype(bf16)
    copies[2].wait()
    x = x_ref[...]
    for z in range(GROUPS):
        o_ref[z, :, 0:BLOCK] = x


def project_kernel(r_ref, filters_ref, o_ref, scratch):
    x = r_ref[:, 0:BLOCK]
    weights = r_ref[:, BLOCK : BLOCK + 128]
    projected = lax.dot_general(
        weights, x, (((0,), (0,)), ((), ())), preferred_element_type=f32
    )
    for j in range(4):
        lanes = slice(128 * j, 128 * (j + 1))
        for g in range(3):
            scratch[pl.ds(4 * g + j, PLANE, stride=CHUNK), :] = projected[
                PLANE * g : PLANE * (g + 1), lanes
            ]
        for f in range(2):
            scratch[pl.ds(12 + 4 * f + j, PLANE, stride=CHUNK), :] = filters_ref[f, :, lanes]
    o_ref[...] = scratch[...].astype(bf16)


def outer_forward(signal, first):
    high, low = split(signal)
    return mm(first[0], jnp.concatenate([high, low], axis=0)) + mm(first[1][:, ROWS:], high)


def inner_forward(stages, twiddle, second):
    reals, imags = [], []
    for stage in stages:
        real, imag = stage[:ROWS], stage[ROWS:]
        reals.append(real * twiddle[0] - imag * twiddle[1])
        imags.append(real * twiddle[1] + imag * twiddle[0])
    real = jnp.concatenate(reals, axis=0)
    imag = jnp.concatenate(imags, axis=0)
    both = right_product(real + imag, second[0])
    out_real = both - right_product(imag, second[2])
    out_imag = both - right_product(real, second[1])
    return [
        (out_real[ROWS * s : ROWS * (s + 1)], out_imag[ROWS * s : ROWS * (s + 1)])
        for s in range(len(stages))
    ]


def inverse(spectrum, last, twiddle, second):
    both = right_product(spectrum[0] + spectrum[1], second[0])
    real = both - right_product(spectrum[1], second[1])
    imag = both - right_product(spectrum[0], second[2])
    turned_real = real * twiddle[0] + imag * twiddle[1]
    turned_imag = imag * twiddle[0] - real * twiddle[1]
    return left_product(last, jnp.concatenate([turned_real, turned_imag], axis=0))


def times(left, right):
    return (left[0] * right[0] - left[1] * right[1], left[0] * right[1] + left[1] * right[0])


def short_filter(blocks, taps, group):
    lane = lax.broadcasted_iota(jnp.int32, (PLANE, COLS), 1)
    chip = lax.broadcasted_iota(jnp.int32, (PLANE, COLS), 0)
    shifted = []
    for by in (1, 2):
        rolled = [pltpu.roll(block, by, 1) for block in blocks]
        before = jnp.where(chip == 0, 0.0, pltpu.roll(rolled[3], 1, 0))
        edges = [before, rolled[0], rolled[1], rolled[2]]
        shifted.append([jnp.where(lane < by, edges[q], rolled[q]) for q in range(4)])
    tap = [taps[group : group + 1, j : j + 1] for j in range(3)]
    return [
        tap[0] * blocks[q] + tap[1] * shifted[0][q] + tap[2] * shifted[1][q] for q in range(4)
    ]


def convolve(core, loaded, taps, gains, first, last, own_last, twiddle, second):
    def classes(array):
        return [
            jnp.concatenate([loaded(q // 2, array, 2 * (q % 2) + h) for h in range(2)], axis=1)
            for q in range(4)
        ]

    groups = [jnp.concatenate(short_filter(classes(g), taps, g), axis=0) for g in range(3)]
    responses = jnp.concatenate(
        [jnp.concatenate(classes(3 + f), axis=0).astype(bf16) for f in range(2)], axis=1
    )
    values, first_gate, second_gate = groups
    pair = mm(first[1], jnp.concatenate([responses, responses], axis=0))
    value_spectrum, first_spectrum, second_spectrum = inner_forward(
        [outer_forward(values, first), pair[:, :COLS], pair[:, COLS:]], twiddle, second
    )
    convolved = inverse(times(value_spectrum, first_spectrum), last, twiddle, second)
    gated = first_gate * (convolved + gains[:, 0:1] * values)
    (gated_spectrum,) = inner_forward([outer_forward(gated, first)], twiddle, second)
    own = inverse(times(gated_spectrum, second_spectrum), own_last, twiddle, second)
    half = ROWS // 2
    own_gated = jnp.where(core == 0, gated[:half], gated[half:])
    own_gate = jnp.where(core == 0, second_gate[:half], second_gate[half:])
    return own_gate * (own + gains[:, 1:2] * own_gated)


def convolve_kernel(
    mine_ref, other_ref, taps_ref, gains_ref, first_ref, last_ref, twiddle_ref, second_ref,
    o_ref, wide, result,
):
    device = lax.axis_index("seq")
    core = device % 2
    channel = device // 2
    half = ROWS // 2
    wide[core] = mine_ref[...].astype(f32)
    wide[1 - core] = other_ref[...].astype(f32)
    mixed = convolve(
        core,
        lambda k, array, j: wide[k, pl.ds(4 * array + j, PLANE, stride=CHUNK), :],
        taps_ref[channel],
        gains_ref[pl.ds(channel, 1), :],
        first_ref,
        last_ref,
        [last_ref[i, pl.ds(pl.multiple_of(half * core, half), half), :] for i in range(2)],
        twiddle_ref,
        second_ref,
    )
    for j in range(4):
        result[pl.ds(j, PLANE, stride=4), :] = mixed[
            PLANE * (j // 2) : PLANE * (j // 2 + 1), 128 * (j % 2) : 128 * (j % 2 + 1)
        ]
    out = result[...].astype(bf16)
    for z in range(GROUPS):
        o_ref[z] = out


def output_kernel(r_ref, weights_ref, o_ref, scratch):
    scratch[...] = r_ref[...].astype(f32)
    mixed = jnp.concatenate(
        [scratch[pl.ds(j, 256, stride=4), :].astype(bf16) for j in range(4)], axis=1
    )
    weights = weights_ref[:, 96:128]
    o_ref[...] = lax.dot_general(
        weights, mixed, (((0,), (0,)), ((), ())), preferred_element_type=f32
    ).astype(bf16)


def grant(mebibytes):
    return pltpu.CompilerParams(vmem_limit_bytes=mebibytes * 1024 * 1024)


def local(inputs, proj_weight, short_taps, skip_gain, filters, out_weight):
    table = tables()
    hbm = pl.BlockSpec(memory_space=pltpu.HBM)
    packed = pl.pallas_call(
        pack_kernel,
        out_shape=jax.ShapeDtypeStruct((GROUPS, 32, BLOCK + 128), bf16),
        in_specs=[hbm] * 3,
        scratch_shapes=[
            pltpu.VMEM((32, BLOCK), bf16),
            pltpu.VMEM((3, 32, 256), bf16),
            pltpu.VMEM((32, 256), bf16),
            pltpu.SemaphoreType.DMA((3,)),
        ],
        compiler_params=grant(4),
        name="pack",
    )(inputs, proj_weight, out_weight)
    gathered = lax.all_to_all(packed, "ch", 0, 0, tiled=True).reshape(256, BLOCK + 128)

    sent = pl.pallas_call(
        project_kernel,
        out_shape=jax.ShapeDtypeStruct((PLANE * CHUNK, 128), bf16),
        scratch_shapes=[pltpu.VMEM((PLANE * CHUNK, 128), f32)],
        compiler_params=grant(8),
        name="project",
    )(gathered, filters)
    same_core = [[2 * c + k for c in range(PLANE)] for k in range(2)]
    mine = lax.all_to_all(
        sent.reshape(PLANE, CHUNK // 4, 4, 128),
        "seq",
        0,
        0,
        tiled=True,
        axis_index_groups=same_core,
    ).reshape(PLANE * CHUNK, 128)
    other = lax.ppermute(mine, "seq", [(i, i ^ 1) for i in range(2 * PLANE)])

    mixed = pl.pallas_call(
        convolve_kernel,
        out_shape=jax.ShapeDtypeStruct((GROUPS, 128, 128), bf16),
        scratch_shapes=[
            pltpu.VMEM((2, PLANE * CHUNK, 128), f32),
            pltpu.VMEM((128, 128), f32),
        ],
        compiler_params=grant(24),
        name="convolve",
    )(
        mine,
        other,
        short_taps,
        skip_gain,
        table["first"],
        table["last"],
        table["twiddle"],
        table["second"],
    )
    everyone = [
        [(2 * c + k) * GROUPS + z for z in range(GROUPS) for c in range(PLANE)] for k in range(2)
    ]
    arrived = lax.all_to_all(
        mixed.reshape(256, 4, 128),
        ("seq", "ch"),
        0,
        0,
        tiled=True,
        axis_index_groups=everyone,
    ).reshape(1024, 128)
    return pl.pallas_call(
        output_kernel,
        out_shape=jax.ShapeDtypeStruct((32, BLOCK), bf16),
        in_specs=[
            pl.BlockSpec((1024, 128), lambda i: (0, 0)),
            pl.BlockSpec((256, 128), lambda i: (0, 4)),
        ],
        out_specs=pl.BlockSpec((32, BLOCK), lambda i: (0, 0)),
        grid=(1,),
        scratch_shapes=[pltpu.VMEM((1024, 128), f32)],
        compiler_params=grant(8),
        name="output",
    )(arrived, gathered)


def solution(mesh):
    in_specs = (
        P("ch", "seq"),
        P(None, "ch", None),
        P("ch", None, None),
        P("ch", None),
        P(None, "ch", "seq"),
        P("ch", None),
    )
    return jax.shard_map(
        local, mesh=mesh, in_specs=in_specs, out_specs=P("ch", "seq"), check_vma=False
    )
```

time: 88.2 us -> 78.4 us (0.89)
  Pallas kernels: 12.4 us -> 4.29 us
  blocking collectives: 67.2 us -> 64.5 us
    pallas_call x1, Pallas kernels: 6.69 us -> 2.93 us  [local(): pl.pallas_call(convolve_kernel, out_shape=jax.ShapeDtypeStruct((GROUPS, 1...]
    pallas_call x1, Pallas kernels: 2.2 us -> 0.21 us  [local(): pl.pallas_call(project_kernel, out_shape=jax.ShapeDtypeStruct((PLANE * CH...]
    all_to_all x1, blocking collectives: 24.4 us -> 22.7 us  [local(): lax.all_to_all(mixed.reshape(256, 4, 128), ('seq', 'ch'), 0, 0, tiled=Tru...]
    pallas_call x1, Pallas kernels: 1.65 us -> 0.27 us  [local(): pl.pallas_call(pack_kernel, out_shape=jax.ShapeDtypeStruct((GROUPS, 32, B...]
    pallas_call x1, Pallas kernels: 1.81 us -> 0.87 us  [local(): pl.pallas_call(output_kernel, out_shape=jax.ShapeDtypeStruct((32, BLOCK),...]
    all_to_all x1, blocking collectives: 20.2 us -> 19.2 us  [local(): lax.all_to_all(sent.reshape(PLANE, CHUNK // 4, 4, 128), 'seq', 0, 0, tile...]
    unnamed x10 -> x22, local copies, waits for them, and re-layouts: 2.13 us -> 2.5 us
  transfers between devices with their start and end apart: 1 -> 1, of which waited for: 0 -> 1; matrix products, arithmetic and copies ran while one was open for 2% -> 0% of each run, Pallas kernels for 0% -> 0%
where the time goes in v2:
time: 78.4 us; the launch traced here: 78 us
  blocking collectives  64.5 us (82%)
  starting transfers between devices  5.84 us (7%)
  Pallas kernels  4.29 us (5%)
  local copies, waits for them, and re-layouts  2.5 us (3%)
  waiting for transfers between devices  0.79 us (1%)
    all_to_all x1, blocking collectives, local(): lax.all_to_all(mixed.reshape(256, 4, 128), ('seq', 'ch'), 0, 0, tiled=Tru...  22.7 us
    all_to_all x1, blocking collectives, local(): lax.all_to_all(packed, 'ch', 0, 0, tiled=True).reshape(256, BLOCK + 128)  22.5 us
    all_to_all x1, blocking collectives, local(): lax.all_to_all(sent.reshape(PLANE, CHUNK // 4, 4, 128), 'seq', 0, 0, tile...  19.2 us
    ppermute x1, starting transfers between devices, local(): other = lax.ppermute(mine, 'seq', [(i, i ^ 1) for i in range(2 * PLANE)])  5.84 us
    pallas_call x1, Pallas kernels, local(): pl.pallas_call(convolve_kernel, out_shape=jax.ShapeDtypeStruct((GROUPS, 1...  2.93 us
    unnamed x22, local copies, waits for them, and re-layouts  2.5 us
  transfers between devices with their start and end apart: 1, of which 1 were waited for; matrix products, arithmetic and copies ran while one was open for 0% of the time, Pallas kernels for 0%

profile of v2, /device:TPU:1, one launch (start us, length us, event | category | flops | bytes accessed | tf_op | source)
XLA Modules:
  0.0 78.0 jit_solution(4783703624553755234)
XLA Ops:
  0.0 0.8 %copy-done.5 = bf16[3,32,256]{2,1,0:T(8,128)(2,1)S(1)} copy-done((bf16[3,32,256]{2,1,0:T(8,128)(2,1)S(1)}, bf16[3,32,256]{2,1,0:T(8,128)(2,1)}, u32[]{:S(2)}) %copy-start.5) | copy-done | bytes 49176
  0.8 0.8 copy-done.6
  1.6 0.7 copy-done.7
  2.3 0.3 pack.1
  2.6 0.0 copy-start
  2.6 22.5 %all_to_all.15 = bf16[8,32,640]{2,1,0:T(8,128)(2,1)S(1)} all-to-all(bf16[8,32,640]{2,1,0:T(8,128)(2,1)S(1)} %pack.1), channel_id=1, replica_groups=mesh['seq'=64,'ch'=8] {'ch'}, dimensions={0} | all-to-all | bytes 655360 | tf_op jit(solution)/shard_map/all_to_all | solution.py:252
  25.1 0.0 copy-done.3
  25.1 0.2 project.1
  25.3 0.0 copy-start.1
  25.4 0.0 copy-start.4
  25.4 19.2 %all_to_all.16 = bf16[32,5,4,128]{3,2,1,0:T(4,128)(2,1)S(1)} all-to-all(bf16[32,5,4,128]{3,2,1,0:T(4,128)(2,1)S(1)} %bitcast.11), channel_id=1, replica_groups={{0,16,32,48,64,80,96,112,128,144,160,176,192,208,224,240,256,272,288,30..., dimensions={0} | all-to-all | bytes 327680 | tf_op jit(solution)/shard_map/all_to_all | solution.py:262
  44.6 5.8 %collective-permute-start = (bf16[640,128]{1,0:T(8,128)(2,1)S(1)}, bf16[640,128]{1,0:T(8,128)(2,1)S(1)}, u32[]{:S(2)}, u32[]{:S(2)}) collective-permute-start(bf16[640,128]{1,0:T(8,128)(2,1)S(1)} %bitcast.9), channel_id=1, source_target_pairs={{0,8},{8,0},{16,24},{24,16},{32,40},{40,32},{48,56},{56,48},{64,72... | collective-permute-start | bytes 491528 | tf_op jit(solution)/shard_map/ppermute | solution.py:270
  50.5 0.0 copy-done.9
  50.5 0.1 copy.12.gains_ref
  50.5 0.0 copy-done.8
  50.6 0.1 copy.11.taps_ref
  50.7 0.8 %collective-permute-done.other_ref = bf16[640,128]{1,0:T(8,128)(2,1)S(1)} collective-permute-done((bf16[640,128]{1,0:T(8,128)(2,1)S(1)}, bf16[640,128]{1,0:T(8,128)(2,1)S(1)}, u32[]{:S(2)}, u32[]{:S(2)}) %collective-permute-start) | collective-permute-done | bytes 163872 | tf_op jit(solution)/shard_map/ppermute | solution.py:270
  51.5 0.0 copy-done
  51.5 0.0 copy-done.2
  51.5 0.0 copy-done.1
  51.5 0.0 copy-done.4
  51.5 2.9 %convolve.1 = bf16[8,128,128]{2,1,0:T(8,128)(2,1)S(1)} custom-call(bf16[640,128]{1,0:T(8,128)(2,1)S(1)} %bitcast.10, bf16[640,128]{1,0:T(8,128)(2,1)S(1)} %collective-permute-done.other_ref, f32[32,3,3]{2,1,0:T(4,128)S(1)} %copy.11.taps_ref, f32[32,2]{1,0:T(8,128)S(1)} %copy.12.gains_ref, bf16[2,256,256]{2,1,0:T(8,128)(2,1)S(1)} %copy-done.2, ...), custom_call_target="tpu_custom_call" | custom-call | tf_op jit(solution)/shard_map/convolve/pallas_call | solution.py:272
  54.4 22.7 %all_to_all.17 = bf16[256,4,128]{2,1,0:T(4,128)(2,1)S(1)} all-to-all(bf16[256,4,128]{2,1,0:T(4,128)(2,1)S(1)} %bitcast.8), channel_id=1, replica_groups={{0,16,32,48,64,80,96,112,128,144,160,176,192,208,224,240,256,272,288,30..., dimensions={0} | all-to-all | bytes 524288 | tf_op jit(solution)/shard_map/all_to_all | solution.py:294
  77.1 0.9 %output.1 = bf16[32,512]{1,0:T(8,128)(2,1)} custom-call(bf16[1024,128]{1,0:T(8,128)(2,1)S(1)} %bitcast.7, bf16[256,640]{1,0:T(8,128)(2,1)S(1)} %bitcast.6), custom_call_target="tpu_custom_call" | custom-call | tf_op jit(solution)/shard_map/output/pallas_call | solution.py:302
  (7 shorter events, 0.0 us)
Async XLA Ops:
  0.0 0.8 %copy-start.5 = (bf16[3,32,256]{2,1,0:T(8,128)(2,1)S(1)}, bf16[3,32,256]{2,1,0:T(8,128)(2,1)}, u32[]{:S(2)}) copy-start(bf16[3,32,256]{2,1,0:T(8,128)(2,1)} %proj_hbm.1) | copy-start | bytes 147460
  0.8 0.8 copy-start.6
  1.6 0.7 copy-start.7
  2.3 22.8 %copy-start.3 = (f32[2,32,512]{2,1,0:T(8,128)S(1)}, f32[2,32,512]{2,1,0:T(8,128)}, u32[]{:S(2)}) copy-start(f32[2,32,512]{2,1,0:T(8,128)} %filters_ref.1) | copy-start | bytes 393220
  2.6 48.9 %copy-start = (bf16[3,2,256,256]{3,2,1,0:T(8,128)(2,1)S(1)}, bf16[3,2,256,256]{3,2,1,0:T(8,128)(2,1)}, u32[]{:S(2)}) copy-start(bf16[3,2,256,256]{3,2,1,0:T(8,128)(2,1)} %constant.11.clone.second_ref) | copy-start | bytes 2359300
  25.1 25.3 %copy-start.9 = (f32[32,2]{0,1:T(2,128)S(1)}, f32[32,2]{0,1:T(2,128)}, u32[]{:S(2)}) copy-start(f32[32,2]{0,1:T(2,128)} %param.13) | copy-start | bytes 772
  25.1 25.4 %copy-start.8 = (f32[32,3,3]{0,2,1:T(4,128)S(1)}, f32[32,3,3]{0,2,1:T(4,128)}, u32[]{:S(2)}) copy-start(f32[32,3,3]{0,2,1:T(4,128)} %param.12) | copy-start | bytes 3460
  25.1 26.4 %copy-start.2 = (bf16[2,256,256]{2,1,0:T(8,128)(2,1)S(1)}, bf16[2,256,256]{2,1,0:T(8,128)(2,1)}, u32[]{:S(2)}) copy-start(bf16[2,256,256]{2,1,0:T(8,128)(2,1)} %constant.8.clone.first_ref) | copy-start | bytes 786436
  25.3 26.1 %copy-start.1 = (f32[2,128,256]{2,1,0:T(8,128)S(1)}, f32[2,128,256]{2,1,0:T(8,128)}, u32[]{:S(2)}) copy-start(f32[2,128,256]{2,1,0:T(8,128)} %constant.10.clone.twiddle_ref) | copy-start | bytes 786436
  25.4 26.1 %copy-start.4 = (bf16[2,128,256]{2,1,0:T(8,128)(2,1)S(1)}, bf16[2,128,256]{2,1,0:T(8,128)(2,1)}, u32[]{:S(2)}) copy-start(bf16[2,128,256]{2,1,0:T(8,128)(2,1)} %constant.9.clone.last_ref) | copy-start | bytes 393220
  44.6 6.9 %collective-permute-start = (bf16[640,128]{1,0:T(8,128)(2,1)S(1)}, bf16[640,128]{1,0:T(8,128)(2,1)S(1)}, u32[]{:S(2)}, u32[]{:S(2)}) collective-permute-start(bf16[640,128]{1,0:T(8,128)(2,1)S(1)} %bitcast.9), channel_id=1, source_target_pairs={{0,8},{8,0},{16,24},{24,16},{32,40},{40,32},{48,56},{56,48},{64,72... | collective-permute-start | bytes 491528 | tf_op jit(solution)/shard_map/ppermute | solution.py:270

commit v3 on v2

--- a/solution.py
+++ b/solution.py
@@ -67,16 +67,19 @@
     return mm(high, table[0]) + mm(low, table[0]) + mm(high, table[1])
 
 
-def pack_kernel(x_hbm, proj_hbm, out_w_hbm, o_ref, x_ref, proj_ref, out_w_ref, sems):
-    copies = [
-        pltpu.make_async_copy(proj_hbm, proj_ref, sems.at[0]),
-        pltpu.make_async_copy(out_w_hbm, out_w_ref, sems.at[1]),
-        pltpu.make_async_copy(x_hbm, x_ref, sems.at[2]),
-    ]
-    for copy in copies:
+def pack_kernel(x_hbm, proj_hbm, out_w_hbm, o_ref, proj_ref, out_w_ref, sems):
+    loads = [
+        pltpu.make_async_copy(proj_hbm, proj_ref, sems.at[GROUPS]),
+        pltpu.make_async_copy(out_w_hbm, out_w_ref, sems.at[GROUPS + 1]),
+    ]
+    spread = [
+        pltpu.make_async_copy(x_hbm, o_ref.at[z, :, pl.ds(0, BLOCK)], sems.at[z])
+        for z in range(GROUPS)
+    ]
+    for copy in loads + spread:
         copy.start()
-    copies[0].wait()
-    copies[1].wait()
+    for copy in loads:
+        copy.wait()
     weights = [proj_ref[g].astype(f32) for g in range(3)] + [out_w_ref[...].astype(f32)]
     lane = lax.broadcasted_iota(jnp.int32, (32, 128), 1) // 32
     for z in range(GROUPS):
@@ -89,10 +92,8 @@
                 piece = pltpu.roll(piece, by, 1)
             picked = piece if picked is None else jnp.where(lane == g, piece, picked)
         o_ref[z, :, BLOCK : BLOCK + 128] = picked.astype(bf16)
-    copies[2].wait()
-    x = x_ref[...]
-    for z in range(GROUPS):
-        o_ref[z, :, 0:BLOCK] = x
+    for copy in spread:
+        copy.wait()
 
 
 def project_kernel(r_ref, filters_ref, o_ref, scratch):
@@ -223,7 +224,7 @@
     mixed = jnp.concatenate(
         [scratch[pl.ds(j, 256, stride=4), :].astype(bf16) for j in range(4)], axis=1
     )
-    weights = weights_ref[:, 96:128]
+    weights = weights_ref[:, BLOCK + 96 : BLOCK + 128]
     o_ref[...] = lax.dot_general(
         weights, mixed, (((0,), (0,)), ((), ())), preferred_element_type=f32
     ).astype(bf16)
@@ -241,14 +242,13 @@
         out_shape=jax.ShapeDtypeStruct((GROUPS, 32, BLOCK + 128), bf16),
         in_specs=[hbm] * 3,
         scratch_shapes=[
-            pltpu.VMEM((32, BLOCK), bf16),
             pltpu.VMEM((3, 32, 256), bf16),
             pltpu.VMEM((32, 256), bf16),
-            pltpu.SemaphoreType.DMA((3,)),
+            pltpu.SemaphoreType.DMA((GROUPS + 2,)),
         ],
         compiler_params=grant(4),
         name="pack",
-    )(inputs, proj_weight, out_weight)
+    )(*(pltpu.with_memory_space_constraint(a, pltpu.HBM) for a in (inputs, proj_weight, out_weight)))
     gathered = lax.all_to_all(packed, "ch", 0, 0, tiled=True).reshape(256, BLOCK + 128)
 
     sent = pl.pallas_call(
@@ -302,12 +302,6 @@
     return pl.pallas_call(
         output_kernel,
         out_shape=jax.ShapeDtypeStruct((32, BLOCK), bf16),
-        in_specs=[
-            pl.BlockSpec((1024, 128), lambda i: (0, 0)),
-            pl.BlockSpec((256, 128), lambda i: (0, 4)),
-        ],
-        out_specs=pl.BlockSpec((32, BLOCK), lambda i: (0, 0)),
-        grid=(1,),
         scratch_shapes=[pltpu.VMEM((1024, 128), f32)],
         compiler_params=grant(8),
         name="output",

time: 78.4 us -> 76.9 us (0.981)
  local copies, waits for them, and re-layouts: 2.5 us -> 0.23 us
  Pallas kernels: 4.29 us -> 5.15 us
    unnamed x22 -> x16, local copies, waits for them, and re-layouts: 2.5 us -> 0.23 us
    pallas_call x1, Pallas kernels: 0.27 us -> 1.13 us  [local(): pl.pallas_call(pack_kernel, out_shape=jax.ShapeDtypeStruct((GROUPS, 32, B...]
where the time goes in v3:
time: 76.9 us; the launch traced here: 76.6 us
  blocking collectives  64.5 us (84%)
  starting transfers between devices  5.84 us (8%)
  Pallas kernels  5.15 us (7%)
  waiting for transfers between devices  0.79 us (1%)
    all_to_all x1, blocking collectives, local(): lax.all_to_all(mixed.reshape(256, 4, 128), ('seq', 'ch'), 0, 0, tiled=Tru...  22.7 us
    all_to_all x1, blocking collectives, local(): lax.all_to_all(packed, 'ch', 0, 0, tiled=True).reshape(256, BLOCK + 128)  22.5 us
    all_to_all x1, blocking collectives, local(): lax.all_to_all(sent.reshape(PLANE, CHUNK // 4, 4, 128), 'seq', 0, 0, tile...  19.2 us
    ppermute x1, starting transfers between devices, local(): other = lax.ppermute(mine, 'seq', [(i, i ^ 1) for i in range(2 * PLANE)])  5.84 us
    pallas_call x1, Pallas kernels, local(): pl.pallas_call(convolve_kernel, out_shape=jax.ShapeDtypeStruct((GROUPS, 1...  2.94 us
  transfers between devices with their start and end apart: 1, of which 1 were waited for; matrix products, arithmetic and copies ran while one was open for 0% of the time, Pallas kernels for 0%

profile of v3, /device:TPU:1, one launch (start us, length us, event | category | flops | bytes accessed | tf_op | source)
XLA Modules:
  0.0 76.6 jit_solution(6609487059542697342)
XLA Ops:
  0.0 0.0 copy-start.3
  0.0 1.1 %pack.1 = bf16[8,32,640]{2,1,0:T(8,128)(2,1)S(1)} custom-call(bf16[32,512]{1,0:T(8,128)(2,1)} %x_hbm.1, bf16[3,32,256]{2,1,0:T(8,128)(2,1)} %proj_hbm.1, bf16[32,256]{1,0:T(8,128)(2,1)} %out_w_hbm.1), custom_call_target="tpu_custom_call" | custom-call | tf_op jit(solution)/shard_map/pack/pallas_call | solution.py:240
  1.1 0.0 copy-start
  1.2 22.5 %all_to_all.15 = bf16[8,32,640]{2,1,0:T(8,128)(2,1)S(1)} all-to-all(bf16[8,32,640]{2,1,0:T(8,128)(2,1)S(1)} %pack.1), channel_id=1, replica_groups=mesh['seq'=64,'ch'=8] {'ch'}, dimensions={0} | all-to-all | bytes 655360 | tf_op jit(solution)/shard_map/all_to_all | solution.py:252
  23.7 0.0 copy-done.3
  23.7 0.0 copy-start.6
  23.7 0.0 copy-start.5
  23.7 0.2 project.1
  23.9 0.0 copy-start.1
  23.9 0.0 copy-start.4
  24.0 19.2 %all_to_all.16 = bf16[32,5,4,128]{3,2,1,0:T(4,128)(2,1)S(1)} all-to-all(bf16[32,5,4,128]{3,2,1,0:T(4,128)(2,1)S(1)} %bitcast.11), channel_id=1, replica_groups={{0,16,32,48,64,80,96,112,128,144,160,176,192,208,224,240,256,272,288,30..., dimensions={0} | all-to-all | bytes 327680 | tf_op jit(solution)/shard_map/all_to_all | solution.py:262
  43.2 5.8 %collective-permute-start = (bf16[640,128]{1,0:T(8,128)(2,1)S(1)}, bf16[640,128]{1,0:T(8,128)(2,1)S(1)}, u32[]{:S(2)}, u32[]{:S(2)}) collective-permute-start(bf16[640,128]{1,0:T(8,128)(2,1)S(1)} %bitcast.9), channel_id=1, source_target_pairs={{0,8},{8,0},{16,24},{24,16},{32,40},{40,32},{48,56},{56,48},{64,72... | collective-permute-start | bytes 491528 | tf_op jit(solution)/shard_map/ppermute | solution.py:270
  49.0 0.0 copy-done.6
  49.1 0.1 copy.12.gains_ref
  49.1 0.0 copy-done.5
  49.1 0.1 copy.11.taps_ref
  49.3 0.8 %collective-permute-done.other_ref = bf16[640,128]{1,0:T(8,128)(2,1)S(1)} collective-permute-done((bf16[640,128]{1,0:T(8,128)(2,1)S(1)}, bf16[640,128]{1,0:T(8,128)(2,1)S(1)}, u32[]{:S(2)}, u32[]{:S(2)}) %collective-permute-start) | collective-permute-done | bytes 163872 | tf_op jit(solution)/shard_map/ppermute | solution.py:270
  50.0 0.0 copy-done
  50.0 0.0 copy-done.2
  50.1 0.0 copy-done.1
  50.1 0.0 copy-done.4
  50.1 2.9 %convolve.1 = bf16[8,128,128]{2,1,0:T(8,128)(2,1)S(1)} custom-call(bf16[640,128]{1,0:T(8,128)(2,1)S(1)} %bitcast.10, bf16[640,128]{1,0:T(8,128)(2,1)S(1)} %collective-permute-done.other_ref, f32[32,3,3]{2,1,0:T(4,128)S(1)} %copy.11.taps_ref, f32[32,2]{1,0:T(8,128)S(1)} %copy.12.gains_ref, bf16[2,256,256]{2,1,0:T(8,128)(2,1)S(1)} %copy-done.2, ...), custom_call_target="tpu_custom_call" | custom-call | tf_op jit(solution)/shard_map/convolve/pallas_call | solution.py:272
  53.0 22.7 %all_to_all.17 = bf16[256,4,128]{2,1,0:T(4,128)(2,1)S(1)} all-to-all(bf16[256,4,128]{2,1,0:T(4,128)(2,1)S(1)} %bitcast.8), channel_id=1, replica_groups={{0,16,32,48,64,80,96,112,128,144,160,176,192,208,224,240,256,272,288,30..., dimensions={0} | all-to-all | bytes 524288 | tf_op jit(solution)/shard_map/all_to_all | solution.py:294
  75.7 0.9 %output.1 = bf16[32,512]{1,0:T(8,128)(2,1)} custom-call(bf16[1024,128]{1,0:T(8,128)(2,1)S(1)} %bitcast.7, bf16[256,640]{1,0:T(8,128)(2,1)S(1)} %bitcast.6), custom_call_target="tpu_custom_call" | custom-call | tf_op jit(solution)/shard_map/output/pallas_call | solution.py:302
  (1 shorter events, 0.0 us)
Async XLA Ops:
  0.0 23.7 %copy-start.3 = (f32[2,32,512]{2,1,0:T(8,128)S(1)}, f32[2,32,512]{2,1,0:T(8,128)}, u32[]{:S(2)}) copy-start(f32[2,32,512]{2,1,0:T(8,128)} %filters_ref.1) | copy-start | bytes 393220
  1.1 48.9 %copy-start = (bf16[3,2,256,256]{3,2,1,0:T(8,128)(2,1)S(1)}, bf16[3,2,256,256]{3,2,1,0:T(8,128)(2,1)}, u32[]{:S(2)}) copy-start(bf16[3,2,256,256]{3,2,1,0:T(8,128)(2,1)} %constant.11.clone.second_ref) | copy-start | bytes 2359300
  23.7 25.3 %copy-start.6 = (f32[32,2]{0,1:T(2,128)S(1)}, f32[32,2]{0,1:T(2,128)}, u32[]{:S(2)}) copy-start(f32[32,2]{0,1:T(2,128)} %param.13) | copy-start | bytes 772
  23.7 25.4 %copy-start.5 = (f32[32,3,3]{0,2,1:T(4,128)S(1)}, f32[32,3,3]{0,2,1:T(4,128)}, u32[]{:S(2)}) copy-start(f32[32,3,3]{0,2,1:T(4,128)} %param.12) | copy-start | bytes 3460
  23.7 26.4 %copy-start.2 = (bf16[2,256,256]{2,1,0:T(8,128)(2,1)S(1)}, bf16[2,256,256]{2,1,0:T(8,128)(2,1)}, u32[]{:S(2)}) copy-start(bf16[2,256,256]{2,1,0:T(8,128)(2,1)} %constant.8.clone.first_ref) | copy-start | bytes 786436
  23.9 26.1 %copy-start.1 = (f32[2,128,256]{2,1,0:T(8,128)S(1)}, f32[2,128,256]{2,1,0:T(8,128)}, u32[]{:S(2)}) copy-start(f32[2,128,256]{2,1,0:T(8,128)} %constant.10.clone.twiddle_ref) | copy-start | bytes 786436
  23.9 26.1 %copy-start.4 = (bf16[2,128,256]{2,1,0:T(8,128)(2,1)S(1)}, bf16[2,128,256]{2,1,0:T(8,128)(2,1)}, u32[]{:S(2)}) copy-start(bf16[2,128,256]{2,1,0:T(8,128)(2,1)} %constant.9.clone.last_ref) | copy-start | bytes 393220
  43.2 6.9 %collective-permute-start = (bf16[640,128]{1,0:T(8,128)(2,1)S(1)}, bf16[640,128]{1,0:T(8,128)(2,1)S(1)}, u32[]{:S(2)}, u32[]{:S(2)}) collective-permute-start(bf16[640,128]{1,0:T(8,128)(2,1)S(1)} %bitcast.9), channel_id=1, source_target_pairs={{0,8},{8,0},{16,24},{24,16},{32,40},{40,32},{48,56},{56,48},{64,72... | collective-permute-start | bytes 491528 | tf_op jit(solution)/shard_map/ppermute | solution.py:270

commit v4 on v3

--- a/solution.py
+++ b/solution.py
@@ -14,6 +14,7 @@
 ROWS = 128
 COLS = 256
 TOTAL = ROWS * COLS
+HALF = COLS // 2
 PLANE = 32
 GROUPS = 8
 BLOCK = 512
@@ -40,8 +41,10 @@
     first = np.concatenate([np.cos(angle), -np.sin(angle)], axis=0)
     column = np.arange(COLS, dtype=np.float64)
     turn = 2.0 * np.pi * ((freq[:, None] * column[None, :]) % (4 * TOTAL)) / (4 * TOTAL)
-    inner = 2.0 * np.pi * ((column[:, None] * column[None, :]) % COLS) / COLS
+    part = column[:HALF]
+    inner = 2.0 * np.pi * ((part[:, None] * part[None, :]) % HALF) / HALF
     cosine, sine = np.cos(inner), np.sin(inner)
+    spin = 2.0 * np.pi * part[None, :] / COLS
     high, low = halves(first)
     return {
         "first": np.stack(
@@ -49,7 +52,8 @@
         ),
         "last": np.stack(halves(first.T / TOTAL)),
         "twiddle": np.stack([np.cos(turn), -np.sin(turn)]).astype(np.float32),
-        "second": np.stack([np.stack(halves(t)) for t in (cosine, cosine + sine, cosine - sine)]),
+        "spin": np.stack([np.cos(spin), -np.sin(spin)]).astype(np.float32),
+        "second": np.stack(halves(np.block([[cosine, -sine], [sine, cosine]]))),
     }
 
 
@@ -118,27 +122,31 @@
     return mm(first[0], jnp.concatenate([high, low], axis=0)) + mm(first[1][:, ROWS:], high)
 
 
-def inner_forward(stages, twiddle, second):
-    reals, imags = [], []
+def inner_forward(stages, twiddle, spin, second):
+    rows = []
     for stage in stages:
         real, imag = stage[:ROWS], stage[ROWS:]
-        reals.append(real * twiddle[0] - imag * twiddle[1])
-        imags.append(real * twiddle[1] + imag * twiddle[0])
-    real = jnp.concatenate(reals, axis=0)
-    imag = jnp.concatenate(imags, axis=0)
-    both = right_product(real + imag, second[0])
-    out_real = both - right_product(imag, second[2])
-    out_imag = both - right_product(real, second[1])
+        turned = (real * twiddle[0] - imag * twiddle[1], real * twiddle[1] + imag * twiddle[0])
+        even = [part[:, :HALF] + part[:, HALF:] for part in turned]
+        odd = [part[:, :HALF] - part[:, HALF:] for part in turned]
+        odd = [odd[0] * spin[0] - odd[1] * spin[1], odd[0] * spin[1] + odd[1] * spin[0]]
+        rows += [jnp.concatenate(even, axis=1), jnp.concatenate(odd, axis=1)]
+    product = right_product(jnp.concatenate(rows, axis=0), second)
     return [
-        (out_real[ROWS * s : ROWS * (s + 1)], out_imag[ROWS * s : ROWS * (s + 1)])
+        (product[2 * ROWS * s : 2 * ROWS * (s + 1), :HALF],
+         product[2 * ROWS * s : 2 * ROWS * (s + 1), HALF:])
         for s in range(len(stages))
     ]
 
 
-def inverse(spectrum, last, twiddle, second):
-    both = right_product(spectrum[0] + spectrum[1], second[0])
-    real = both - right_product(spectrum[1], second[1])
-    imag = both - right_product(spectrum[0], second[2])
+def inverse(spectrum, last, twiddle, spin, second):
+    product = right_product(jnp.concatenate([spectrum[1], spectrum[0]], axis=1), second)
+    even_imag, even_real = product[:ROWS, :HALF], product[:ROWS, HALF:]
+    odd_imag, odd_real = product[ROWS:, :HALF], product[ROWS:, HALF:]
+    spun_real = odd_real * spin[0] + odd_imag * spin[1]
+    spun_imag = odd_imag * spin[0] - odd_real * spin[1]
+    real = jnp.concatenate([even_real + spun_real, even_real - spun_real], axis=1)
+    imag = jnp.concatenate([even_imag + spun_imag, even_imag - spun_imag], axis=1)
     turned_real = real * twiddle[0] + imag * twiddle[1]
     turned_imag = imag * twiddle[0] - real * twiddle[1]
     return left_product(last, jnp.concatenate([turned_real, turned_imag], axis=0))
@@ -163,7 +171,7 @@
     ]
 
 
-def convolve(core, loaded, taps, gains, first, last, own_last, twiddle, second):
+def convolve(core, loaded, taps, gains, first, last, own_last, twiddle, spin, second):
     def classes(array):
         return [
             jnp.concatenate([loaded(q // 2, array, 2 * (q % 2) + h) for h in range(2)], axis=1)
@@ -176,13 +184,14 @@
     )
     values, first_gate, second_gate = groups
     pair = mm(first[1], jnp.concatenate([responses, responses], axis=0))
-    value_spectrum, first_spectrum, second_spectrum = inner_forward(
-        [outer_forward(values, first), pair[:, :COLS], pair[:, COLS:]], twiddle, second
-    )
-    convolved = inverse(times(value_spectrum, first_spectrum), last, twiddle, second)
+    value_spectrum, first_spectrum = inner_forward(
+        [outer_forward(values, first), pair[:, :COLS]], twiddle, spin, second
+    )
+    (second_spectrum,) = inner_forward([pair[:, COLS:]], twiddle, spin, second)
+    convolved = inverse(times(value_spectrum, first_spectrum), last, twiddle, spin, second)
     gated = first_gate * (convolved + gains[:, 0:1] * values)
-    (gated_spectrum,) = inner_forward([outer_forward(gated, first)], twiddle, second)
-    own = inverse(times(gated_spectrum, second_spectrum), own_last, twiddle, second)
+    (gated_spectrum,) = inner_forward([outer_forward(gated, first)], twiddle, spin, second)
+    own = inverse(times(gated_spectrum, second_spectrum), own_last, twiddle, spin, second)
     half = ROWS // 2
     own_gated = jnp.where(core == 0, gated[:half], gated[half:])
     own_gate = jnp.where(core == 0, second_gate[:half], second_gate[half:])
@@ -190,8 +199,8 @@
 
 
 def convolve_kernel(
-    mine_ref, other_ref, taps_ref, gains_ref, first_ref, last_ref, twiddle_ref, second_ref,
-    o_ref, wide, result,
+    mine_ref, other_ref, taps_ref, gains_ref, first_ref, last_ref, twiddle_ref, spin_ref,
+    second_ref, o_ref, wide, result,
 ):
     device = lax.axis_index("seq")
     core = device % 2
@@ -208,6 +217,7 @@
         last_ref,
         [last_ref[i, pl.ds(pl.multiple_of(half * core, half), half), :] for i in range(2)],
         twiddle_ref,
+        spin_ref,
         second_ref,
     )
     for j in range(4):
@@ -286,6 +296,7 @@
         table["first"],
         table["last"],
         table["twiddle"],
+        table["spin"],
         table["second"],
     )
     everyone = [

time: 76.9 us -> 76.7 us (level)
  no operation moved by 1% of the time
where the time goes in v4:
time: 76.7 us; the launch traced here: 76.3 us
  blocking collectives  64.5 us (84%)
  starting transfers between devices  5.84 us (8%)
  Pallas kernels  4.88 us (6%)
  waiting for transfers between devices  0.79 us (1%)
    all_to_all x1, blocking collectives, local(): lax.all_to_all(mixed.reshape(256, 4, 128), ('seq', 'ch'), 0, 0, tiled=Tru...  22.7 us
    all_to_all x1, blocking collectives, local(): lax.all_to_all(packed, 'ch', 0, 0, tiled=True).reshape(256, BLOCK + 128)  22.5 us
    all_to_all x1, blocking collectives, local(): lax.all_to_all(sent.reshape(PLANE, CHUNK // 4, 4, 128), 'seq', 0, 0, tile...  19.2 us
    ppermute x1, starting transfers between devices, local(): other = lax.ppermute(mine, 'seq', [(i, i ^ 1) for i in range(2 * PLANE)])  5.84 us
    pallas_call x1, Pallas kernels, local(): pl.pallas_call(convolve_kernel, out_shape=jax.ShapeDtypeStruct((GROUPS, 1...  2.67 us
  transfers between devices with their start and end apart: 1, of which 1 were waited for; matrix products, arithmetic and copies ran while one was open for 0% of the time, Pallas kernels for 0%

profile of v4, /device:TPU:1, one launch (start us, length us, event | category | flops | bytes accessed | tf_op | source)
XLA Modules:
  0.0 76.3 jit_solution(442623711777948638)
XLA Ops:
  0.0 1.1 %pack.1 = bf16[8,32,640]{2,1,0:T(8,128)(2,1)S(1)} custom-call(bf16[32,512]{1,0:T(8,128)(2,1)} %x_hbm.1, bf16[3,32,256]{2,1,0:T(8,128)(2,1)} %proj_hbm.1, bf16[32,256]{1,0:T(8,128)(2,1)} %out_w_hbm.1), custom_call_target="tpu_custom_call" | custom-call | tf_op jit(solution)/shard_map/pack/pallas_call | solution.py:250
  1.1 0.0 copy-start.3
  1.2 22.5 %all_to_all.15 = bf16[8,32,640]{2,1,0:T(8,128)(2,1)S(1)} all-to-all(bf16[8,32,640]{2,1,0:T(8,128)(2,1)S(1)} %pack.1), channel_id=1, replica_groups=mesh['seq'=64,'ch'=8] {'ch'}, dimensions={0} | all-to-all | bytes 655360 | tf_op jit(solution)/shard_map/all_to_all | solution.py:262
  23.7 0.0 copy-done.3
  23.7 0.0 copy-start.7
  23.7 0.0 copy-start.2
  23.7 0.2 project.1
  23.9 0.0 copy-start
  24.0 0.0 copy-start.4
  24.0 19.2 %all_to_all.16 = bf16[32,5,4,128]{3,2,1,0:T(4,128)(2,1)S(1)} all-to-all(bf16[32,5,4,128]{3,2,1,0:T(4,128)(2,1)S(1)} %bitcast.9), channel_id=1, replica_groups={{0,16,32,48,64,80,96,112,128,144,160,176,192,208,224,240,256,272,288,30..., dimensions={0} | all-to-all | bytes 327680 | tf_op jit(solution)/shard_map/all_to_all | solution.py:272
  43.2 5.8 %collective-permute-start = (bf16[640,128]{1,0:T(8,128)(2,1)S(1)}, bf16[640,128]{1,0:T(8,128)(2,1)S(1)}, u32[]{:S(2)}, u32[]{:S(2)}) collective-permute-start(bf16[640,128]{1,0:T(8,128)(2,1)S(1)} %bitcast.10), channel_id=1, source_target_pairs={{0,8},{8,0},{16,24},{24,16},{32,40},{40,32},{48,56},{56,48},{64,72... | collective-permute-start | bytes 491528 | tf_op jit(solution)/shard_map/ppermute | solution.py:280
  49.1 0.0 copy-done.7
  49.1 0.1 copy.13.gains_ref
  49.2 0.0 copy-done.6
  49.2 0.1 copy.12.taps_ref
  49.3 0.8 %collective-permute-done.other_ref = bf16[640,128]{1,0:T(8,128)(2,1)S(1)} collective-permute-done((bf16[640,128]{1,0:T(8,128)(2,1)S(1)}, bf16[640,128]{1,0:T(8,128)(2,1)S(1)}, u32[]{:S(2)}, u32[]{:S(2)}) %collective-permute-start) | collective-permute-done | bytes 163872 | tf_op jit(solution)/shard_map/ppermute | solution.py:280
  50.1 0.0 copy-done.1
  50.1 0.0 copy-done.2
  50.1 0.0 copy-done
  50.1 0.0 copy-done.4
  50.1 0.0 copy-done.5
  50.1 2.7 %convolve.1 = bf16[8,128,128]{2,1,0:T(8,128)(2,1)S(1)} custom-call(bf16[640,128]{1,0:T(8,128)(2,1)S(1)} %bitcast.11, bf16[640,128]{1,0:T(8,128)(2,1)S(1)} %collective-permute-done.other_ref, f32[32,3,3]{2,1,0:T(4,128)S(1)} %copy.12.taps_ref, f32[32,2]{1,0:T(8,128)S(1)} %copy.13.gains_ref, bf16[2,256,256]{2,1,0:T(8,128)(2,1)S(1)} %copy-done.2, ...), custom_call_target="tpu_custom_call" | custom-call | tf_op jit(solution)/shard_map/convolve/pallas_call | solution.py:282
  52.8 22.7 %all_to_all.17 = bf16[256,4,128]{2,1,0:T(4,128)(2,1)S(1)} all-to-all(bf16[256,4,128]{2,1,0:T(4,128)(2,1)S(1)} %bitcast.8), channel_id=1, replica_groups={{0,16,32,48,64,80,96,112,128,144,160,176,192,208,224,240,256,272,288,30..., dimensions={0} | all-to-all | bytes 524288 | tf_op jit(solution)/shard_map/all_to_all | solution.py:305
  75.5 0.9 %output.1 = bf16[32,512]{1,0:T(8,128)(2,1)} custom-call(bf16[1024,128]{1,0:T(8,128)(2,1)S(1)} %bitcast.7, bf16[256,640]{1,0:T(8,128)(2,1)S(1)} %bitcast.6), custom_call_target="tpu_custom_call" | custom-call | tf_op jit(solution)/shard_map/output/pallas_call | solution.py:313
  (3 shorter events, 0.0 us)
Async XLA Ops:
  1.1 22.6 %copy-start.3 = (f32[2,32,512]{2,1,0:T(8,128)S(1)}, f32[2,32,512]{2,1,0:T(8,128)}, u32[]{:S(2)}) copy-start(f32[2,32,512]{2,1,0:T(8,128)} %filters_ref.1) | copy-start | bytes 393220
  23.7 25.4 %copy-start.7 = (f32[32,2]{0,1:T(2,128)S(1)}, f32[32,2]{0,1:T(2,128)}, u32[]{:S(2)}) copy-start(f32[32,2]{0,1:T(2,128)} %param.14) | copy-start | bytes 772
  23.7 25.5 %copy-start.6 = (f32[32,3,3]{0,2,1:T(4,128)S(1)}, f32[32,3,3]{0,2,1:T(4,128)}, u32[]{:S(2)}) copy-start(f32[32,3,3]{0,2,1:T(4,128)} %param.13) | copy-start | bytes 3460
  23.7 26.4 %copy-start.1 = (f32[2,128,256]{2,1,0:T(8,128)S(1)}, f32[2,128,256]{2,1,0:T(8,128)}, u32[]{:S(2)}) copy-start(f32[2,128,256]{2,1,0:T(8,128)} %constant.12.clone.twiddle_ref) | copy-start | bytes 786436
  23.7 26.4 %copy-start.2 = (bf16[2,256,256]{2,1,0:T(8,128)(2,1)S(1)}, bf16[2,256,256]{2,1,0:T(8,128)(2,1)}, u32[]{:S(2)}) copy-start(bf16[2,256,256]{2,1,0:T(8,128)(2,1)} %constant.10.clone.first_ref) | copy-start | bytes 786436
  23.9 26.1 %copy-start = (bf16[2,256,256]{2,1,0:T(8,128)(2,1)S(1)}, bf16[2,256,256]{2,1,0:T(8,128)(2,1)}, u32[]{:S(2)}) copy-start(bf16[2,256,256]{2,1,0:T(8,128)(2,1)} %constant.14.clone.second_ref) | copy-start | bytes 786436
  24.0 26.1 %copy-start.4 = (bf16[2,128,256]{2,1,0:T(8,128)(2,1)S(1)}, bf16[2,128,256]{2,1,0:T(8,128)(2,1)}, u32[]{:S(2)}) copy-start(bf16[2,128,256]{2,1,0:T(8,128)(2,1)} %constant.11.clone.last_ref) | copy-start | bytes 393220
  43.2 6.9 %collective-permute-start = (bf16[640,128]{1,0:T(8,128)(2,1)S(1)}, bf16[640,128]{1,0:T(8,128)(2,1)S(1)}, u32[]{:S(2)}, u32[]{:S(2)}) collective-permute-start(bf16[640,128]{1,0:T(8,128)(2,1)S(1)} %bitcast.10), channel_id=1, source_target_pairs={{0,8},{8,0},{16,24},{24,16},{32,40},{40,32},{48,56},{56,48},{64,72... | collective-permute-start | bytes 491528 | tf_op jit(solution)/shard_map/ppermute | solution.py:280
  49.2 0.9 %copy-start.5 = (f32[2,1,128]{2,1,0:T(1,128)S(1)}, f32[2,1,128]{2,1,0:T(1,128)}, u32[]{:S(2)}) copy-start(f32[2,1,128]{2,1,0:T(1,128)} %constant.13.clone.spin_ref) | copy-start | bytes 3076

commit v5 on v4

--- a/solution.py
+++ b/solution.py
@@ -7,6 +7,7 @@
 from jax.experimental import pallas as pl
 from jax.experimental.pallas import tpu as pltpu
 from jax.sharding import PartitionSpec as P
+
 
 bf16 = jnp.bfloat16
 f32 = jnp.float32
@@ -234,10 +235,12 @@
     mixed = jnp.concatenate(
         [scratch[pl.ds(j, 256, stride=4), :].astype(bf16) for j in range(4)], axis=1
     )
-    weights = weights_ref[:, BLOCK + 96 : BLOCK + 128]
-    o_ref[...] = lax.dot_general(
-        weights, mixed, (((0,), (0,)), ((), ())), preferred_element_type=f32
-    ).astype(bf16)
+    o_ref[...] = mm(weights_ref[...], mixed).astype(bf16)
+
+
+def turn_kernel(r_ref, o_ref):
+    weights = r_ref[:, BLOCK : BLOCK + 128].astype(f32)
+    o_ref[...] = weights.T[96:128].astype(bf16)
 
 
 def grant(mebibytes):
@@ -309,14 +312,21 @@
         0,
         tiled=True,
         axis_index_groups=everyone,
-    ).reshape(1024, 128)
+    )
+    turned = pl.pallas_call(
+        turn_kernel,
+        out_shape=jax.ShapeDtypeStruct((32, 256), bf16),
+        compiler_params=grant(4),
+        cost_estimate=pl.CostEstimate(flops=1000000, bytes_accessed=1000000, transcendentals=0),
+        name="turn",
+    )(gathered)
     return pl.pallas_call(
         output_kernel,
         out_shape=jax.ShapeDtypeStruct((32, BLOCK), bf16),
         scratch_shapes=[pltpu.VMEM((1024, 128), f32)],
         compiler_params=grant(8),
         name="output",
-    )(arrived, gathered)
+    )(arrived.reshape(1024, 128), turned)
 
 
 def solution(mesh):

time: 76.7 us -> 77.5 us (1.010)
  blocking collectives: 64.5 us -> 41.8 us
  waiting for transfers between devices: 0.79 us -> 14.2 us
  starting transfers between devices: 5.84 us -> 15 us
    all_to_all x1 -> x0, blocking collectives: 22.7 us -> none  [local(): lax.all_to_all(mixed.reshape(256, 4, 128), ('seq', 'ch'), 0, 0, tiled=Tru...]
    all_to_all x0 -> x1, waiting for transfers between devices: none -> 13.4 us  [local(): lax.all_to_all(mixed.reshape(256, 4, 128), ('seq', 'ch'), 0, 0, tiled=Tru...]
    all_to_all x0 -> x1, starting transfers between devices: none -> 9.12 us  [local(): lax.all_to_all(mixed.reshape(256, 4, 128), ('seq', 'ch'), 0, 0, tiled=Tru...]
  transfers between devices with their start and end apart: 1 -> 2, of which waited for: 1 -> 2; matrix products, arithmetic and copies ran while one was open for 0% -> 0% of each run, Pallas kernels for 0% -> 0%
where the time goes in v5:
time: 77.5 us; the launch traced here: 76.9 us
  blocking collectives  41.8 us (54%)
  starting transfers between devices  15 us (19%)
  waiting for transfers between devices  14.2 us (18%)
  Pallas kernels  5.63 us (7%)
    all_to_all x1, blocking collectives, local(): lax.all_to_all(packed, 'ch', 0, 0, tiled=True).reshape(256, BLOCK + 128)  22.5 us
    all_to_all x1, blocking collectives, local(): lax.all_to_all(sent.reshape(PLANE, CHUNK // 4, 4, 128), 'seq', 0, 0, tile...  19.2 us
    all_to_all x1, waiting for transfers between devices, local(): lax.all_to_all(mixed.reshape(256, 4, 128), ('seq', 'ch'), 0, 0, tiled=Tru...  13.4 us
    all_to_all x1, starting transfers between devices, local(): lax.all_to_all(mixed.reshape(256, 4, 128), ('seq', 'ch'), 0, 0, tiled=Tru...  9.12 us
    ppermute x1, starting transfers between devices, local(): other = lax.ppermute(mine, 'seq', [(i, i ^ 1) for i in range(2 * PLANE)])  5.84 us
    pallas_call x1, Pallas kernels, local(): pl.pallas_call(convolve_kernel, out_shape=jax.ShapeDtypeStruct((GROUPS, 1...  3.39 us
  transfers between devices with their start and end apart: 2, of which 2 were waited for; matrix products, arithmetic and copies ran while one was open for 0% of the time, Pallas kernels for 0%

profile of v5, /device:TPU:1, one launch (start us, length us, event | category | flops | bytes accessed | tf_op | source)
XLA Modules:
  0.0 76.9 jit_solution(11617189578542481179)
XLA Ops:
  0.0 1.1 %pack.1 = bf16[8,32,640]{2,1,0:T(8,128)(2,1)S(1)} custom-call(bf16[32,512]{1,0:T(8,128)(2,1)} %x_hbm.1, bf16[3,32,256]{2,1,0:T(8,128)(2,1)} %proj_hbm.1, bf16[32,256]{1,0:T(8,128)(2,1)} %out_w_hbm.1), custom_call_target="tpu_custom_call" | custom-call | tf_op jit(solution)/shard_map/pack/pallas_call | solution.py:253
  1.1 0.0 copy-start.3
  1.2 22.5 %all_to_all.15 = bf16[8,32,640]{2,1,0:T(8,128)(2,1)S(1)} all-to-all(bf16[8,32,640]{2,1,0:T(8,128)(2,1)S(1)} %pack.1), channel_id=1, replica_groups=mesh['seq'=64,'ch'=8] {'ch'}, dimensions={0} | all-to-all | bytes 655360 | tf_op jit(solution)/shard_map/all_to_all | solution.py:265
  23.7 0.0 copy-done.3
  23.7 0.0 copy-start.2
  23.7 0.2 project.1
  23.9 0.0 copy-start
  24.0 0.0 copy-start.4
  24.0 19.2 %all_to_all.16 = bf16[32,5,4,128]{3,2,1,0:T(4,128)(2,1)S(1)} all-to-all(bf16[32,5,4,128]{3,2,1,0:T(4,128)(2,1)S(1)} %bitcast.8), channel_id=1, replica_groups={{0,16,32,48,64,80,96,112,128,144,160,176,192,208,224,240,256,272,288,30..., dimensions={0} | all-to-all | bytes 327680 | tf_op jit(solution)/shard_map/all_to_all | solution.py:275
  43.2 5.8 %collective-permute-start = (bf16[640,128]{1,0:T(8,128)(2,1)S(1)}, bf16[640,128]{1,0:T(8,128)(2,1)S(1)}, u32[]{:S(2)}, u32[]{:S(2)}) collective-permute-start(bf16[640,128]{1,0:T(8,128)(2,1)S(1)} %bitcast.9), channel_id=1, source_target_pairs={{0,8},{8,0},{16,24},{24,16},{32,40},{40,32},{48,56},{56,48},{64,72... | collective-permute-start | bytes 491528 | tf_op jit(solution)/shard_map/ppermute | solution.py:283
  49.1 0.0 copy-done.7
  49.1 0.1 copy.13.gains_ref
  49.2 0.0 copy-done.6
  49.2 0.1 copy.12.taps_ref
  49.3 0.8 %collective-permute-done.other_ref = bf16[640,128]{1,0:T(8,128)(2,1)S(1)} collective-permute-done((bf16[640,128]{1,0:T(8,128)(2,1)S(1)}, bf16[640,128]{1,0:T(8,128)(2,1)S(1)}, u32[]{:S(2)}, u32[]{:S(2)}) %collective-permute-start) | collective-permute-done | bytes 163872 | tf_op jit(solution)/shard_map/ppermute | solution.py:283
  50.1 0.0 copy-done.1
  50.1 0.0 copy-done.2
  50.1 0.0 copy-done.4
  50.1 0.0 copy-done.5
  50.1 3.4 %convolve.1 = bf16[8,128,128]{2,1,0:T(8,128)(2,1)} custom-call(bf16[640,128]{1,0:T(8,128)(2,1)S(1)} %bitcast.10, bf16[640,128]{1,0:T(8,128)(2,1)S(1)} %collective-permute-done.other_ref, f32[32,3,3]{2,1,0:T(4,128)S(1)} %copy.12.taps_ref, f32[32,2]{1,0:T(8,128)S(1)} %copy.13.gains_ref, bf16[2,256,256]{2,1,0:T(8,128)(2,1)S(1)} %copy-done.2, ...), custom_call_target="tpu_custom_call" | custom-call | tf_op jit(solution)/shard_map/convolve/pallas_call | solution.py:285
  53.5 9.1 %all-to-all-start.2 = ((bf16[256,4,128]{2,1,0:T(4,128)(2,1)}), bf16[256,4,128]{2,1,0:T(4,128)(2,1)S(1)}, u32[]{:S(2)}, u32[]{:S(2)}) async-start(bf16[256,4,128]{2,1,0:T(4,128)(2,1)} %bitcast.3), calls=%async_computation.2 | async-start | bytes 524288 | tf_op jit(solution)/shard_map/all_to_all | solution.py:308
  62.6 0.1 turn.1.weights_ref
  62.7 13.4 %all-to-all-done.2 = bf16[256,4,128]{2,1,0:T(4,128)(2,1)S(1)} async-done(((bf16[256,4,128]{2,1,0:T(4,128)(2,1)}), bf16[256,4,128]{2,1,0:T(4,128)(2,1)S(1)}, u32[]{:S(2)}, u32[]{:S(2)}) %all-to-all-start.2) | async-done | bytes 262176 | tf_op jit(solution)/shard_map/all_to_all | solution.py:308
  76.1 0.8 %output.1 = bf16[32,512]{1,0:T(8,128)(2,1)} custom-call(bf16[1024,128]{1,0:T(8,128)(2,1)S(1)} %bitcast.7, bf16[32,256]{1,0:T(8,128)(2,1)S(1)} %turn.1.weights_ref), custom_call_target="tpu_custom_call" | custom-call | tf_op jit(solution)/shard_map/output/pallas_call | solution.py:323
  (5 shorter events, 0.0 us)
Async XLA Ops:
  1.1 22.6 %copy-start.3 = (f32[2,32,512]{2,1,0:T(8,128)S(1)}, f32[2,32,512]{2,1,0:T(8,128)}, u32[]{:S(2)}) copy-start(f32[2,32,512]{2,1,0:T(8,128)} %filters_ref.1) | copy-start | bytes 393220
  23.7 25.4 %copy-start.7 = (f32[32,2]{0,1:T(2,128)S(1)}, f32[32,2]{0,1:T(2,128)}, u32[]{:S(2)}) copy-start(f32[32,2]{0,1:T(2,128)} %param.14) | copy-start | bytes 772
  23.7 25.5 %copy-start.6 = (f32[32,3,3]{0,2,1:T(4,128)S(1)}, f32[32,3,3]{0,2,1:T(4,128)}, u32[]{:S(2)}) copy-start(f32[32,3,3]{0,2,1:T(4,128)} %param.13) | copy-start | bytes 3460
  23.7 26.4 %copy-start.1 = (f32[2,128,256]{2,1,0:T(8,128)S(1)}, f32[2,128,256]{2,1,0:T(8,128)}, u32[]{:S(2)}) copy-start(f32[2,128,256]{2,1,0:T(8,128)} %constant.12.clone.twiddle_ref) | copy-start | bytes 786436
  23.7 26.4 %copy-start.2 = (bf16[2,256,256]{2,1,0:T(8,128)(2,1)S(1)}, bf16[2,256,256]{2,1,0:T(8,128)(2,1)}, u32[]{:S(2)}) copy-start(bf16[2,256,256]{2,1,0:T(8,128)(2,1)} %constant.10.clone.first_ref) | copy-start | bytes 786436
  23.9 26.1 %copy-start = (bf16[2,256,256]{2,1,0:T(8,128)(2,1)S(1)}, bf16[2,256,256]{2,1,0:T(8,128)(2,1)}, u32[]{:S(2)}) copy-start(bf16[2,256,256]{2,1,0:T(8,128)(2,1)} %constant.14.clone.second_ref) | copy-start | bytes 786436
  24.0 26.1 %copy-start.4 = (bf16[2,128,256]{2,1,0:T(8,128)(2,1)S(1)}, bf16[2,128,256]{2,1,0:T(8,128)(2,1)}, u32[]{:S(2)}) copy-start(bf16[2,128,256]{2,1,0:T(8,128)(2,1)} %constant.11.clone.last_ref) | copy-start | bytes 393220
  43.2 6.9 %collective-permute-start = (bf16[640,128]{1,0:T(8,128)(2,1)S(1)}, bf16[640,128]{1,0:T(8,128)(2,1)S(1)}, u32[]{:S(2)}, u32[]{:S(2)}) collective-permute-start(bf16[640,128]{1,0:T(8,128)(2,1)S(1)} %bitcast.9), channel_id=1, source_target_pairs={{0,8},{8,0},{16,24},{24,16},{32,40},{40,32},{48,56},{56,48},{64,72... | collective-permute-start | bytes 491528 | tf_op jit(solution)/shard_map/ppermute | solution.py:283
  49.2 0.9 %copy-start.5 = (f32[2,1,128]{2,1,0:T(1,128)S(1)}, f32[2,1,128]{2,1,0:T(1,128)}, u32[]{:S(2)}) copy-start(f32[2,1,128]{2,1,0:T(1,128)} %constant.13.clone.spin_ref) | copy-start | bytes 3076
  53.5 22.6 %all-to-all-start.2 = ((bf16[256,4,128]{2,1,0:T(4,128)(2,1)}), bf16[256,4,128]{2,1,0:T(4,128)(2,1)S(1)}, u32[]{:S(2)}, u32[]{:S(2)}) async-start(bf16[256,4,128]{2,1,0:T(4,128)(2,1)} %bitcast.3), calls=%async_computation.2 | async-start | bytes 524288 | tf_op jit(solution)/shard_map/all_to_all | solution.py:308

commit v6 on v4

--- a/solution.py
+++ b/solution.py
@@ -67,8 +67,11 @@
 
 
 def right_product(values, table):
-    high, low = split(values)
-    return mm(high, table[0]) + mm(low, table[0]) + mm(high, table[1])
+    parts = []
+    for at in range(0, values.shape[0], 128):
+        high, low = split(values[at : at + 128])
+        parts.append(mm(high, table[0]) + mm(low, table[0]) + mm(high, table[1]))
+    return jnp.concatenate(parts, axis=0)
 
 
 def pack_kernel(x_hbm, proj_hbm, out_w_hbm, o_ref, proj_ref, out_w_ref, sems):

time: 76.7 us -> 76.5 us (level)
  no operation moved by 1% of the time
where the time goes in v6:
time: 76.5 us; the launch traced here: 76.1 us
  blocking collectives  64.5 us (84%)
  starting transfers between devices  5.84 us (8%)
  Pallas kernels  4.66 us (6%)
  waiting for transfers between devices  0.79 us (1%)
    all_to_all x1, blocking collectives, local(): lax.all_to_all(mixed.reshape(256, 4, 128), ('seq', 'ch'), 0, 0, tiled=Tru...  22.7 us
    all_to_all x1, blocking collectives, local(): lax.all_to_all(packed, 'ch', 0, 0, tiled=True).reshape(256, BLOCK + 128)  22.5 us
    all_to_all x1, blocking collectives, local(): lax.all_to_all(sent.reshape(PLANE, CHUNK // 4, 4, 128), 'seq', 0, 0, tile...  19.2 us
    ppermute x1, starting transfers between devices, local(): other = lax.ppermute(mine, 'seq', [(i, i ^ 1) for i in range(2 * PLANE)])  5.84 us
    pallas_call x1, Pallas kernels, local(): pl.pallas_call(convolve_kernel, out_shape=jax.ShapeDtypeStruct((GROUPS, 1...  2.45 us
  transfers between devices with their start and end apart: 1, of which 1 were waited for; matrix products, arithmetic and copies ran while one was open for 0% of the time, Pallas kernels for 0%

profile of v6, /device:TPU:1, one launch (start us, length us, event | category | flops | bytes accessed | tf_op | source)
XLA Modules:
  0.0 76.1 jit_solution(8796025566044235723)
XLA Ops:
  0.0 1.1 %pack.1 = bf16[8,32,640]{2,1,0:T(8,128)(2,1)S(1)} custom-call(bf16[32,512]{1,0:T(8,128)(2,1)} %x_hbm.1, bf16[3,32,256]{2,1,0:T(8,128)(2,1)} %proj_hbm.1, bf16[32,256]{1,0:T(8,128)(2,1)} %out_w_hbm.1), custom_call_target="tpu_custom_call" | custom-call | tf_op jit(solution)/shard_map/pack/pallas_call | solution.py:253
  1.1 0.0 copy-start.3
  1.2 22.5 %all_to_all.15 = bf16[8,32,640]{2,1,0:T(8,128)(2,1)S(1)} all-to-all(bf16[8,32,640]{2,1,0:T(8,128)(2,1)S(1)} %pack.1), channel_id=1, replica_groups=mesh['seq'=64,'ch'=8] {'ch'}, dimensions={0} | all-to-all | bytes 655360 | tf_op jit(solution)/shard_map/all_to_all | solution.py:265
  23.7 0.0 copy-done.3
  23.7 0.0 copy-start.7
  23.7 0.0 copy-start.2
  23.7 0.2 project.1
  23.9 0.0 copy-start
  24.0 0.0 copy-start.4
  24.0 19.2 %all_to_all.16 = bf16[32,5,4,128]{3,2,1,0:T(4,128)(2,1)S(1)} all-to-all(bf16[32,5,4,128]{3,2,1,0:T(4,128)(2,1)S(1)} %bitcast.9), channel_id=1, replica_groups={{0,16,32,48,64,80,96,112,128,144,160,176,192,208,224,240,256,272,288,30..., dimensions={0} | all-to-all | bytes 327680 | tf_op jit(solution)/shard_map/all_to_all | solution.py:275
  43.2 5.8 %collective-permute-start = (bf16[640,128]{1,0:T(8,128)(2,1)S(1)}, bf16[640,128]{1,0:T(8,128)(2,1)S(1)}, u32[]{:S(2)}, u32[]{:S(2)}) collective-permute-start(bf16[640,128]{1,0:T(8,128)(2,1)S(1)} %bitcast.10), channel_id=1, source_target_pairs={{0,8},{8,0},{16,24},{24,16},{32,40},{40,32},{48,56},{56,48},{64,72... | collective-permute-start | bytes 491528 | tf_op jit(solution)/shard_map/ppermute | solution.py:283
  49.1 0.0 copy-done.7
  49.1 0.1 copy.13.gains_ref
  49.2 0.0 copy-done.6
  49.2 0.1 copy.12.taps_ref
  49.3 0.8 %collective-permute-done.other_ref = bf16[640,128]{1,0:T(8,128)(2,1)S(1)} collective-permute-done((bf16[640,128]{1,0:T(8,128)(2,1)S(1)}, bf16[640,128]{1,0:T(8,128)(2,1)S(1)}, u32[]{:S(2)}, u32[]{:S(2)}) %collective-permute-start) | collective-permute-done | bytes 163872 | tf_op jit(solution)/shard_map/ppermute | solution.py:283
  50.1 0.0 copy-done.1
  50.1 0.0 copy-done.2
  50.1 0.0 copy-done
  50.1 0.0 copy-done.4
  50.1 0.0 copy-done.5
  50.1 2.4 %convolve.1 = bf16[8,128,128]{2,1,0:T(8,128)(2,1)S(1)} custom-call(bf16[640,128]{1,0:T(8,128)(2,1)S(1)} %bitcast.11, bf16[640,128]{1,0:T(8,128)(2,1)S(1)} %collective-permute-done.other_ref, f32[32,3,3]{2,1,0:T(4,128)S(1)} %copy.12.taps_ref, f32[32,2]{1,0:T(8,128)S(1)} %copy.13.gains_ref, bf16[2,256,256]{2,1,0:T(8,128)(2,1)S(1)} %copy-done.2, ...), custom_call_target="tpu_custom_call" | custom-call | tf_op jit(solution)/shard_map/convolve/pallas_call | solution.py:285
  52.5 22.7 %all_to_all.17 = bf16[256,4,128]{2,1,0:T(4,128)(2,1)S(1)} all-to-all(bf16[256,4,128]{2,1,0:T(4,128)(2,1)S(1)} %bitcast.8), channel_id=1, replica_groups={{0,16,32,48,64,80,96,112,128,144,160,176,192,208,224,240,256,272,288,30..., dimensions={0} | all-to-all | bytes 524288 | tf_op jit(solution)/shard_map/all_to_all | solution.py:308
  75.3 0.9 %output.1 = bf16[32,512]{1,0:T(8,128)(2,1)} custom-call(bf16[1024,128]{1,0:T(8,128)(2,1)S(1)} %bitcast.7, bf16[256,640]{1,0:T(8,128)(2,1)S(1)} %bitcast.6), custom_call_target="tpu_custom_call" | custom-call | tf_op jit(solution)/shard_map/output/pallas_call | solution.py:316
  (3 shorter events, 0.0 us)
Async XLA Ops:
  1.1 22.6 %copy-start.3 = (f32[2,32,512]{2,1,0:T(8,128)S(1)}, f32[2,32,512]{2,1,0:T(8,128)}, u32[]{:S(2)}) copy-start(f32[2,32,512]{2,1,0:T(8,128)} %filters_ref.1) | copy-start | bytes 393220
  23.7 25.4 %copy-start.7 = (f32[32,2]{0,1:T(2,128)S(1)}, f32[32,2]{0,1:T(2,128)}, u32[]{:S(2)}) copy-start(f32[32,2]{0,1:T(2,128)} %param.14) | copy-start | bytes 772
  23.7 25.5 %copy-start.6 = (f32[32,3,3]{0,2,1:T(4,128)S(1)}, f32[32,3,3]{0,2,1:T(4,128)}, u32[]{:S(2)}) copy-start(f32[32,3,3]{0,2,1:T(4,128)} %param.13) | copy-start | bytes 3460
  23.7 26.4 %copy-start.1 = (f32[2,128,256]{2,1,0:T(8,128)S(1)}, f32[2,128,256]{2,1,0:T(8,128)}, u32[]{:S(2)}) copy-start(f32[2,128,256]{2,1,0:T(8,128)} %constant.12.clone.twiddle_ref) | copy-start | bytes 786436
  23.7 26.4 %copy-start.2 = (bf16[2,256,256]{2,1,0:T(8,128)(2,1)S(1)}, bf16[2,256,256]{2,1,0:T(8,128)(2,1)}, u32[]{:S(2)}) copy-start(bf16[2,256,256]{2,1,0:T(8,128)(2,1)} %constant.10.clone.first_ref) | copy-start | bytes 786436
  23.9 26.1 %copy-start = (bf16[2,256,256]{2,1,0:T(8,128)(2,1)S(1)}, bf16[2,256,256]{2,1,0:T(8,128)(2,1)}, u32[]{:S(2)}) copy-start(bf16[2,256,256]{2,1,0:T(8,128)(2,1)} %constant.14.clone.second_ref) | copy-start | bytes 786436
  24.0 26.1 %copy-start.4 = (bf16[2,128,256]{2,1,0:T(8,128)(2,1)S(1)}, bf16[2,128,256]{2,1,0:T(8,128)(2,1)}, u32[]{:S(2)}) copy-start(bf16[2,128,256]{2,1,0:T(8,128)(2,1)} %constant.11.clone.last_ref) | copy-start | bytes 393220
  43.2 6.9 %collective-permute-start = (bf16[640,128]{1,0:T(8,128)(2,1)S(1)}, bf16[640,128]{1,0:T(8,128)(2,1)S(1)}, u32[]{:S(2)}, u32[]{:S(2)}) collective-permute-start(bf16[640,128]{1,0:T(8,128)(2,1)S(1)} %bitcast.10), channel_id=1, source_target_pairs={{0,8},{8,0},{16,24},{24,16},{32,40},{40,32},{48,56},{56,48},{64,72... | collective-permute-start | bytes 491528 | tf_op jit(solution)/shard_map/ppermute | solution.py:283
  49.2 0.9 %copy-start.5 = (f32[2,1,128]{2,1,0:T(1,128)S(1)}, f32[2,1,128]{2,1,0:T(1,128)}, u32[]{:S(2)}) copy-start(f32[2,1,128]{2,1,0:T(1,128)} %constant.13.clone.spin_ref) | copy-start | bytes 3076

commit v7 on v6

--- a/solution.py
+++ b/solution.py
@@ -103,12 +103,10 @@
         copy.wait()
 
 
-def project_kernel(r_ref, filters_ref, o_ref, scratch):
-    x = r_ref[:, 0:BLOCK]
-    weights = r_ref[:, BLOCK : BLOCK + 128]
-    projected = lax.dot_general(
-        weights, x, (((0,), (0,)), ((), ())), preferred_element_type=f32
-    )
+def project_kernel(r_ref, filters_ref, o_ref, out_w_ref, scratch):
+    weights = r_ref[:, BLOCK : BLOCK + 128].astype(f32).T.astype(bf16)
+    out_w_ref[...] = weights[96:128]
+    projected = mm(weights[0:96], r_ref[:, 0:BLOCK])
     for j in range(4):
         lanes = slice(128 * j, 128 * (j + 1))
         for g in range(3):
@@ -181,11 +179,12 @@
             for q in range(4)
         ]
 
-    groups = [jnp.concatenate(short_filter(classes(g), taps, g), axis=0) for g in range(3)]
+    values, first_gate = [
+        jnp.concatenate(short_filter(classes(g), taps, g), axis=0) for g in range(2)
+    ]
     responses = jnp.concatenate(
         [jnp.concatenate(classes(3 + f), axis=0).astype(bf16) for f in range(2)], axis=1
     )
-    values, first_gate, second_gate = groups
     pair = mm(first[1], jnp.concatenate([responses, responses], axis=0))
     value_spectrum, first_spectrum = inner_forward(
         [outer_forward(values, first), pair[:, :COLS]], twiddle, spin, second
@@ -197,7 +196,22 @@
     own = inverse(times(gated_spectrum, second_spectrum), own_last, twiddle, spin, second)
     half = ROWS // 2
     own_gated = jnp.where(core == 0, gated[:half], gated[half:])
-    own_gate = jnp.where(core == 0, second_gate[:half], second_gate[half:])
+    lane = lax.broadcasted_iota(jnp.int32, (PLANE, COLS), 1)
+    chip = lax.broadcasted_iota(jnp.int32, (PLANE, COLS), 0)
+    near = [
+        jnp.concatenate([loaded(core, 2, 2 * r + h) for h in range(2)], axis=1) for r in range(2)
+    ]
+    far = jnp.concatenate([loaded(1 - core, 2, 2 + h) for h in range(2)], axis=1)
+    tap = [taps[2:3, j : j + 1] for j in range(3)]
+    own_gate = [tap[0] * near[0], tap[0] * near[1]]
+    for by in (1, 2):
+        edge = pltpu.roll(far, by, 1)
+        down = jnp.where(chip == 0, 0.0, pltpu.roll(edge, 1, 0))
+        edge = jnp.where(core == 0, down, edge)
+        rolled = [pltpu.roll(part, by, 1) for part in near]
+        own_gate[0] += tap[by] * jnp.where(lane < by, edge, rolled[0])
+        own_gate[1] += tap[by] * jnp.where(lane < by, rolled[0], rolled[1])
+    own_gate = jnp.concatenate(own_gate, axis=0)
     return own_gate * (own + gains[:, 1:2] * own_gated)
 
 
@@ -237,10 +251,7 @@
     mixed = jnp.concatenate(
         [scratch[pl.ds(j, 256, stride=4), :].astype(bf16) for j in range(4)], axis=1
     )
-    weights = weights_ref[:, BLOCK + 96 : BLOCK + 128]
-    o_ref[...] = lax.dot_general(
-        weights, mixed, (((0,), (0,)), ((), ())), preferred_element_type=f32
-    ).astype(bf16)
+    o_ref[...] = mm(weights_ref[...], mixed).astype(bf16)
 
 
 def grant(mebibytes):
@@ -264,9 +275,12 @@
     )(*(pltpu.with_memory_space_constraint(a, pltpu.HBM) for a in (inputs, proj_weight, out_weight)))
     gathered = lax.all_to_all(packed, "ch", 0, 0, tiled=True).reshape(256, BLOCK + 128)
 
-    sent = pl.pallas_call(
+    sent, turned = pl.pallas_call(
         project_kernel,
-        out_shape=jax.ShapeDtypeStruct((PLANE * CHUNK, 128), bf16),
+        out_shape=(
+            jax.ShapeDtypeStruct((PLANE * CHUNK, 128), bf16),
+            jax.ShapeDtypeStruct((32, 256), bf16),
+        ),
         scratch_shapes=[pltpu.VMEM((PLANE * CHUNK, 128), f32)],
         compiler_params=grant(8),
         name="project",
@@ -319,7 +333,7 @@
         scratch_shapes=[pltpu.VMEM((1024, 128), f32)],
         compiler_params=grant(8),
         name="output",
-    )(arrived, gathered)
+    )(arrived, turned)
 
 
 def solution(mesh):

time: 76.5 us -> 76.5 us (level)
  no operation moved by 1% of the time
where the time goes in v7:
time: 76.5 us; the launch traced here: 76.2 us
  blocking collectives  64.5 us (84%)
  starting transfers between devices  5.97 us (8%)
  Pallas kernels  4.62 us (6%)
  waiting for transfers between devices  0.77 us (1%)
    all_to_all x1, blocking collectives, local(): lax.all_to_all(mixed.reshape(256, 4, 128), ('seq', 'ch'), 0, 0, tiled=Tru...  22.7 us
    all_to_all x1, blocking collectives, local(): lax.all_to_all(packed, 'ch', 0, 0, tiled=True).reshape(256, BLOCK + 128)  22.5 us
    all_to_all x1, blocking collectives, local(): lax.all_to_all(sent.reshape(PLANE, CHUNK // 4, 4, 128), 'seq', 0, 0, tile...  19.2 us
    ppermute x1, starting transfers between devices, local(): other = lax.ppermute(mine, 'seq', [(i, i ^ 1) for i in range(2 * PLANE)])  5.97 us
    pallas_call x1, Pallas kernels, local(): pl.pallas_call(convolve_kernel, out_shape=jax.ShapeDtypeStruct((GROUPS, 1...  2.45 us
  transfers between devices with their start and end apart: 1, of which 1 were waited for; matrix products, arithmetic and copies ran while one was open for 0% of the time, Pallas kernels for 0%

profile of v7, /device:TPU:1, one launch (start us, length us, event | category | flops | bytes accessed | tf_op | source)
XLA Modules:
  0.0 76.2 jit_solution(4045839076005914220)
XLA Ops:
  0.0 1.1 %pack.1 = bf16[8,32,640]{2,1,0:T(8,128)(2,1)S(1)} custom-call(bf16[32,512]{1,0:T(8,128)(2,1)} %x_hbm.1, bf16[3,32,256]{2,1,0:T(8,128)(2,1)} %proj_hbm.1, bf16[32,256]{1,0:T(8,128)(2,1)} %out_w_hbm.1), custom_call_target="tpu_custom_call" | custom-call | tf_op jit(solution)/shard_map/pack/pallas_call | solution.py:264
  1.1 0.0 copy-start.3
  1.2 0.0 copy-start.4
  1.2 22.5 %all_to_all.15 = bf16[8,32,640]{2,1,0:T(8,128)(2,1)S(1)} all-to-all(bf16[8,32,640]{2,1,0:T(8,128)(2,1)S(1)} %pack.1), channel_id=1, replica_groups=mesh['seq'=64,'ch'=8] {'ch'}, dimensions={0} | all-to-all | bytes 655360 | tf_op jit(solution)/shard_map/all_to_all | solution.py:276
  23.7 0.0 copy-done.3
  23.7 0.0 copy-start.6
  23.7 0.2 project.1
  24.0 0.0 copy-start
  24.0 19.2 %all_to_all.16 = bf16[32,5,4,128]{3,2,1,0:T(4,128)(2,1)S(1)} all-to-all(bf16[32,5,4,128]{3,2,1,0:T(4,128)(2,1)S(1)} %bitcast.10), channel_id=1, replica_groups={{0,16,32,48,64,80,96,112,128,144,160,176,192,208,224,240,256,272,288,30..., dimensions={0} | all-to-all | bytes 327680 | tf_op jit(solution)/shard_map/all_to_all | solution.py:289
  43.2 6.0 %collective-permute-start = (bf16[640,128]{1,0:T(8,128)(2,1)S(1)}, bf16[640,128]{1,0:T(8,128)(2,1)S(1)}, u32[]{:S(2)}, u32[]{:S(2)}) collective-permute-start(bf16[640,128]{1,0:T(8,128)(2,1)S(1)} %bitcast.8), channel_id=1, source_target_pairs={{0,8},{8,0},{16,24},{24,16},{32,40},{40,32},{48,56},{56,48},{64,72... | collective-permute-start | bytes 491528 | tf_op jit(solution)/shard_map/ppermute | solution.py:297
  49.2 0.0 copy-done.6
  49.2 0.1 copy.12.taps_ref
  49.3 0.0 copy-done.7
  49.3 0.0 copy-start.5
  49.3 0.1 copy.13.gains_ref
  49.4 0.8 %collective-permute-done.other_ref = bf16[640,128]{1,0:T(8,128)(2,1)S(1)} collective-permute-done((bf16[640,128]{1,0:T(8,128)(2,1)S(1)}, bf16[640,128]{1,0:T(8,128)(2,1)S(1)}, u32[]{:S(2)}, u32[]{:S(2)}) %collective-permute-start) | collective-permute-done | bytes 163872 | tf_op jit(solution)/shard_map/ppermute | solution.py:297
  50.2 0.0 copy-done.4
  50.2 0.0 copy-done.1
  50.2 0.0 copy-done.2
  50.2 0.0 copy-done
  50.2 0.0 copy-done.5
  50.2 2.4 %convolve.1 = bf16[8,128,128]{2,1,0:T(8,128)(2,1)S(1)} custom-call(bf16[640,128]{1,0:T(8,128)(2,1)S(1)} %bitcast.9, bf16[640,128]{1,0:T(8,128)(2,1)S(1)} %collective-permute-done.other_ref, f32[32,3,3]{2,1,0:T(4,128)S(1)} %copy.12.taps_ref, f32[32,2]{1,0:T(8,128)S(1)} %copy.13.gains_ref, bf16[2,256,256]{2,1,0:T(8,128)(2,1)S(1)} %copy-done, ...), custom_call_target="tpu_custom_call" | custom-call | tf_op jit(solution)/shard_map/convolve/pallas_call | solution.py:299
  52.7 22.7 %all_to_all.17 = bf16[256,4,128]{2,1,0:T(4,128)(2,1)S(1)} all-to-all(bf16[256,4,128]{2,1,0:T(4,128)(2,1)S(1)} %bitcast.7), channel_id=1, replica_groups={{0,16,32,48,64,80,96,112,128,144,160,176,192,208,224,240,256,272,288,30..., dimensions={0} | all-to-all | bytes 524288 | tf_op jit(solution)/shard_map/all_to_all | solution.py:322
  75.4 0.8 %output.1 = bf16[32,512]{1,0:T(8,128)(2,1)} custom-call(bf16[1024,128]{1,0:T(8,128)(2,1)S(1)} %bitcast.6, bf16[32,256]{1,0:T(8,128)(2,1)S(1)} %get-tuple-element.8.weights_ref), custom_call_target="tpu_custom_call" | custom-call | tf_op jit(solution)/shard_map/output/pallas_call | solution.py:330
  (3 shorter events, 0.0 us)
Async XLA Ops:
  1.1 22.6 %copy-start.3 = (f32[2,32,512]{2,1,0:T(8,128)S(1)}, f32[2,32,512]{2,1,0:T(8,128)}, u32[]{:S(2)}) copy-start(f32[2,32,512]{2,1,0:T(8,128)} %filters_ref.1) | copy-start | bytes 393220
  1.2 49.0 %copy-start.4 = (bf16[2,128,256]{2,1,0:T(8,128)(2,1)S(1)}, bf16[2,128,256]{2,1,0:T(8,128)(2,1)}, u32[]{:S(2)}) copy-start(bf16[2,128,256]{2,1,0:T(8,128)(2,1)} %constant.11.clone.last_ref) | copy-start | bytes 393220
  23.7 25.5 %copy-start.6 = (f32[32,3,3]{0,2,1:T(4,128)S(1)}, f32[32,3,3]{0,2,1:T(4,128)}, u32[]{:S(2)}) copy-start(f32[32,3,3]{0,2,1:T(4,128)} %param.13) | copy-start | bytes 3460
  23.7 26.5 %copy-start.1 = (f32[2,128,256]{2,1,0:T(8,128)S(1)}, f32[2,128,256]{2,1,0:T(8,128)}, u32[]{:S(2)}) copy-start(f32[2,128,256]{2,1,0:T(8,128)} %constant.12.clone.twiddle_ref) | copy-start | bytes 786436
  23.7 26.5 %copy-start.2 = (bf16[2,256,256]{2,1,0:T(8,128)(2,1)S(1)}, bf16[2,256,256]{2,1,0:T(8,128)(2,1)}, u32[]{:S(2)}) copy-start(bf16[2,256,256]{2,1,0:T(8,128)(2,1)} %constant.14.clone.second_ref) | copy-start | bytes 786436
  24.0 26.2 %copy-start = (bf16[2,256,256]{2,1,0:T(8,128)(2,1)S(1)}, bf16[2,256,256]{2,1,0:T(8,128)(2,1)}, u32[]{:S(2)}) copy-start(bf16[2,256,256]{2,1,0:T(8,128)(2,1)} %constant.10.clone.first_ref) | copy-start | bytes 786436
  43.2 6.1 %copy-start.7 = (f32[32,2]{0,1:T(2,128)S(1)}, f32[32,2]{0,1:T(2,128)}, u32[]{:S(2)}) copy-start(f32[32,2]{0,1:T(2,128)} %param.14) | copy-start | bytes 772
  43.2 7.0 %collective-permute-start = (bf16[640,128]{1,0:T(8,128)(2,1)S(1)}, bf16[640,128]{1,0:T(8,128)(2,1)S(1)}, u32[]{:S(2)}, u32[]{:S(2)}) collective-permute-start(bf16[640,128]{1,0:T(8,128)(2,1)S(1)} %bitcast.8), channel_id=1, source_target_pairs={{0,8},{8,0},{16,24},{24,16},{32,40},{40,32},{48,56},{56,48},{64,72... | collective-permute-start | bytes 491528 | tf_op jit(solution)/shard_map/ppermute | solution.py:297
  49.3 0.9 %copy-start.5 = (f32[2,1,128]{2,1,0:T(1,128)S(1)}, f32[2,1,128]{2,1,0:T(1,128)}, u32[]{:S(2)}) copy-start(f32[2,1,128]{2,1,0:T(1,128)} %constant.13.clone.spin_ref) | copy-start | bytes 3076
